TPU v7x, 32 devices: a whole 2x2x4 slice. The times are simulated.
32 devices in a mesh: band: 8 (over z, x), tile: 4 (over y, core).
Axes of the slice: x: 2, y: 2, z: 4, core: 2. Of those that a mesh axis runs over, the one named last changes fastest.
Arguments:
- source: bfloat16 [40, 262144], P(None, ('band', 'tile')), may hold values from -6 to 6
- regrid_weights: bfloat16 [2048, 4, 128, 128], P(('band', 'tile')), may hold values from -0.5 to 0.5
- dest_group: int32 [2048, 4], P(('band', 'tile')), may hold values from 0 to 31, all different within a row; in each aligned block of 64 rows (0 to 63, 64 to 127, ...) at most 24 rows name the same one
- dest_block: int32 [2048, 4], P(('band', 'tile')), may hold values from 0 to 767
- seam_table: int32 [12, 4, 3], replicated, may hold values from 0 to 11, as said below
- conv1_weight: bfloat16 [9, 128, 40], replicated, may hold values from -0.3125 to 0.3125
- conv1_bias: float32 [128], replicated, may hold values from -3 to 3
- conv2_weight: bfloat16 [9, 128, 128], replicated, may hold values from -0.1875 to 0.1875
- conv2_bias: float32 [128], replicated, may hold values from -3 to 3
Outputs:
- features: bfloat16 [128, 12, 512, 512], P(None, None, 'band', 'tile')
Inputs may be any that keep to these rules, and one draw needn't show every extreme that they name: `dest_group`: within the rows of one device (aligned blocks of 64 rows) no value appears more than 24 times, and a row's 4 values differ. `seam_table`: entries 0 and 1 name a face and a side (0 to 3). Joins are symmetric: if side s of face f is joined to side s2 of face g, side s2 of face g is joined to side s of face f with the same reversal entry. No side is joined to itself. Entry 2 is 0 or 1.
All inputs are finite; a program needn't handle non-finite values.
Results may differ from a plain program's by a relative error of at most 0.0058.
Values may be sent and summed in bfloat16 or wider, within the bound.
A program may use at most 640 MiB of HBM per device.

v0:
```python
import jax
import jax.numpy as jnp
from jax import lax
from jax.sharding import PartitionSpec as P


def with_halo(shard, sides, width):
    for axis, dim in sides:
        size, length = (lax.axis_size(axis), shard.shape[dim])
        up = [(i, (i + 1) % size) for i in range(size - 1)]
        down = [(j, i) for i, j in up]
        last = lax.slice_in_dim(shard, length - width, length, axis=dim)
        leading = lax.slice_in_dim(shard, 0, width, axis=dim)
        before = lax.ppermute(last, axis, up)
        after = lax.ppermute(leading, axis, down)
        shard = jnp.concatenate([before, shard, after], axis=dim)
    return shard


def seam_fill(padded, tile_data, seam_table):
    channels, face_count, rows_dev, cols_dev = tile_data.shape
    band_count = lax.axis_size("band")
    tile_count = lax.axis_size("tile")
    side_len = cols_dev * tile_count
    band_pos = lax.axis_index("band")
    tile_pos = lax.axis_index("tile")
    line_index = (seam_table[:, :, 0] * 4 + seam_table[:, :, 1]).reshape(-1)
    reverse = (seam_table[:, :, 2] == 1).reshape(-1)[None, :, None]
    zero_line = jnp.zeros((channels, face_count, side_len), jnp.float32)
    first_band = (band_pos == 0).astype(jnp.float32)
    last_band = (band_pos == band_count - 1).astype(jnp.float32)
    first_tile = (tile_pos == 0).astype(jnp.float32)
    last_tile = (tile_pos == tile_count - 1).astype(jnp.float32)
    top_part = lax.dynamic_update_slice_in_dim(
        zero_line, tile_data[:, :, 0, :].astype(jnp.float32) * first_band, tile_pos * cols_dev, 2
    )
    bottom_part = lax.dynamic_update_slice_in_dim(
        zero_line, tile_data[:, :, -1, :].astype(jnp.float32) * last_band, tile_pos * cols_dev, 2
    )
    left_part = lax.dynamic_update_slice_in_dim(
        zero_line, tile_data[:, :, :, 0].astype(jnp.float32) * first_tile, band_pos * rows_dev, 2
    )
    right_part = lax.dynamic_update_slice_in_dim(
        zero_line, tile_data[:, :, :, -1].astype(jnp.float32) * last_tile, band_pos * rows_dev, 2
    )
    own_edges = jnp.stack((top_part, bottom_part, left_part, right_part), axis=2).reshape(
        channels, face_count * 4, side_len
    )
    chosen = own_edges[:, line_index, :]
    chosen = jnp.where(reverse, jnp.flip(chosen, axis=2), chosen)
    seam_lines = lax.psum(chosen, ("band", "tile")).astype(jnp.bfloat16)
    seam_lines = seam_lines.reshape(channels, face_count, 4, side_len)
    padded_lines = jnp.pad(seam_lines, ((0, 0), (0, 0), (0, 0), (1, 1)))
    top_seg = lax.dynamic_slice_in_dim(
        padded_lines[:, :, 0, :], tile_pos * cols_dev, cols_dev + 2, 2
    )
    bottom_seg = lax.dynamic_slice_in_dim(
        padded_lines[:, :, 1, :], tile_pos * cols_dev, cols_dev + 2, 2
    )
    left_seg = lax.dynamic_slice_in_dim(
        padded_lines[:, :, 2, :], band_pos * rows_dev, rows_dev + 2, 2
    )
    right_seg = lax.dynamic_slice_in_dim(
        padded_lines[:, :, 3, :], band_pos * rows_dev, rows_dev + 2, 2
    )
    padded = padded.at[:, :, 0, :].set(jnp.where(band_pos == 0, top_seg, padded[:, :, 0, :]))
    padded = padded.at[:, :, -1, :].set(
        jnp.where(band_pos == band_count - 1, bottom_seg, padded[:, :, -1, :])
    )
    padded = padded.at[:, :, :, 0].set(jnp.where(tile_pos == 0, left_seg, padded[:, :, :, 0]))
    padded = padded.at[:, :, :, -1].set(
        jnp.where(tile_pos == tile_count - 1, right_seg, padded[:, :, :, -1])
    )
    return padded


def conv_layer(tile_data, weight, bias_row, seam_table):
    rows_dev = tile_data.shape[2]
    cols_dev = tile_data.shape[3]
    padded = with_halo(tile_data, (("band", 2), ("tile", 3)), 1)
    padded = seam_fill(padded, tile_data, seam_table)
    summed = jnp.zeros((weight.shape[1], tile_data.shape[1], rows_dev, cols_dev), jnp.float32)
    for row_off in range(3):
        for col_off in range(3):
            window = padded[:, :, row_off : row_off + rows_dev, col_off : col_off + cols_dev]
            summed = summed + jnp.einsum(
                "oi,ifrc->ofrc",
                weight[3 * row_off + col_off],
                window,
                preferred_element_type=jnp.float32,
            )
    return jax.nn.gelu(summed + bias_row[:, None, None, None], approximate=False).astype(
        jnp.bfloat16
    )


def local(
    source,
    regrid_weights,
    dest_group,
    dest_block,
    seam_table,
    conv1_weight,
    conv1_bias,
    conv2_weight,
    conv2_bias,
):
    fields = source.shape[0]
    src_count = regrid_weights.shape[0]
    top_count = regrid_weights.shape[1]
    block_len = regrid_weights.shape[2]
    band_count = lax.axis_size("band")
    tile_count = lax.axis_size("tile")
    devices = band_count * tile_count
    capacity = 3 * src_count * top_count // devices
    rows_dev = block_len * tile_count // band_count
    face_count = seam_table.shape[0]
    slots_dev = face_count * rows_dev
    blocks = source.reshape(fields, src_count, block_len)
    partial_value = jnp.einsum(
        "fsc,skcd->skfd", blocks, regrid_weights, preferred_element_type=jnp.float32
    ).astype(jnp.bfloat16)
    item_count = src_count * top_count
    partial_value = partial_value.reshape(item_count, fields, block_len)
    target_dev = dest_group.reshape(item_count)
    target_slot = dest_block.reshape(item_count)
    onehot_dev = (target_dev[:, None] == jnp.arange(devices, dtype=jnp.int32)[None, :]).astype(
        jnp.int32
    )
    before = jnp.cumsum(onehot_dev, axis=0) - onehot_dev
    rank_in = jnp.sum(before * onehot_dev, axis=1)
    position = target_dev * capacity + rank_in
    outgoing = (
        jnp.zeros((devices * capacity, fields, block_len), jnp.bfloat16)
        .at[position]
        .set(partial_value)
    )
    out_slots = jnp.full((devices * capacity,), slots_dev, jnp.int32).at[position].set(target_slot)
    arrived, arrived_slots = (
        lax.all_to_all(
            outgoing.reshape(devices, capacity, fields, block_len),
            ("band", "tile"),
            split_axis=0,
            concat_axis=0,
            tiled=True,
        ),
        lax.all_to_all(
            out_slots.reshape(devices, capacity),
            ("band", "tile"),
            split_axis=0,
            concat_axis=0,
            tiled=True,
        ),
    )
    arrived = arrived.reshape(devices * capacity, fields, block_len)
    arrived_slots = arrived_slots.reshape(devices * capacity)
    selector = (jnp.arange(slots_dev, dtype=jnp.int32)[:, None] == arrived_slots[None, :]).astype(
        jnp.bfloat16
    )
    regridded = jnp.einsum(
        "tn,nfd->ftd", selector, arrived, preferred_element_type=jnp.float32
    ).astype(jnp.bfloat16)
    regridded = regridded.reshape(fields, face_count, rows_dev, block_len)
    hidden = conv_layer(regridded, conv1_weight, conv1_bias, seam_table)
    return conv_layer(hidden, conv2_weight, conv2_bias, seam_table)


def solution(mesh):
    return jax.shard_map(
        local,
        mesh=mesh,
        in_specs=(
            P(None, ("band", "tile")),
            P(("band", "tile"), None, None, None),
            P(("band", "tile"), None),
            P(("band", "tile"), None),
            P(),
            P(),
            P(),
            P(),
            P(),
        ),
        out_specs=P(None, None, "band", "tile"),
        check_vma=False,
    )
```

profile of v0, /device:TPU:1, one launch (start us, length us, event | category | flops | bytes accessed | tf_op | source)
XLA Modules:
  0.0 1859.3 jit_solution(18389202105939182563)
XLA Ops:
  23.3 29.3 %scatter_fusion = bf16[768,40,128]{2,1,0:T(8,128)(2,1)} fusion(bf16[768,40,128]{2,1,0:T(8,128)(2,1)} %broadcast_in_dim.36, s32[256]{0:T(256)S(1)} %bitcast.354, bf16[256,40,128]{2,1,0:T(8,128)(2,1)S(1)} %bitcast.347), kind=kCustom, calls=%fused_computation.2 | custom fusion | bytes 7865344 | tf_op jit(solution)/shard_map/scatter | solution.py:136
  61.1 171.0 %all-to-all-done = bf16[32,24,40,128]{3,2,1,0:T(8,128)(2,1)} async-done(((bf16[32,24,40,128]{3,2,1,0:T(8,128)(2,1)}), bf16[32,24,40,128]{3,2,1,0:T(8,128)(2,1)}, u32[]{:S(2)}, u32[]{:S(2)}) %all-to-all-start) | async-done | bytes 7864352 | tf_op jit(solution)/shard_map/all_to_all | solution.py:140
  265.7 12.9 fusion.132
  318.7 94.5 %all-reduce.4 = bf16[40,48,512]{2,0,1:T(8,128)(2,1)S(1)} all-reduce(f32[40,48,512]{2,0,1:T(8,128)} %broadcast_select_fusion.1), channel_id=1, replica_groups=mesh['band'=8,'tile'=4] {'band','tile'}, use_global_device_ids=true, to_apply=%region_5.6 | all-reduce | flops 983040 | bytes 5898240 | tf_op jit(solution)/shard_map/psum | solution.py:51
  476.7 18.2 pad_maximum_fusion.1
  504.7 49.0 %scatter.46 = bf16[40,12,66,130]{3,0,2,1:T(8,128)(2,1)} dynamic-update-slice(bf16[40,12,66,130]{3,0,2,1:T(8,128)(2,1)} %copy-done.1, bf16[40,12,66,1]{3,0,2,1:T(8,128)(2,1)} %slice_select_fusion.1, s32[]{:T(128)} %constant.262.clone.1, s32[]{:T(128)} %constant.262.clone.1, s32[]{:T(128)} %constant.262.clone.1, s32[]{:T(128)} %constant.262.clone.1) | dynamic-update-slice | bytes 126724 | tf_op jit(solution)/shard_map/scatter | solution.py:70
  561.5 87.7 %scatter.49 = bf16[40,12,66,130]{3,0,2,1:T(8,128)(2,1)} dynamic-update-slice(bf16[40,12,66,130]{3,0,2,1:T(8,128)(2,1)} %scatter.46, bf16[40,12,66,1]{3,0,2,1:T(8,128)(2,1)} %slice_select_fusion, s32[]{:T(128)} %constant.262.clone.1, s32[]{:T(128)} %constant.262.clone.1, s32[]{:T(128)} %constant.262.clone.1, s32[]{:T(128)} %constant.278.clone.1) | dynamic-update-slice | bytes 126724 | tf_op jit(solution)/shard_map/scatter | solution.py:71
  649.3 24.0 %fusion.57 = f32[12,64,128,128]{3,2,1,0:T(8,128)} fusion(bf16[40,12,66,130]{3,0,2,1:T(8,128)(2,1)} %scatter.49, bf16[9,128,40]{1,2,0:T(8,128)(2,1)S(1)} %copy-done.5), kind=kOutput, calls=%fused_computation.79 | convolution fusion | flops 1006632960 | bytes 58206208 | tf_op jit(solution)/shard_map/oi,ifrc->ofrc/dot_general | solution.py:86
  673.3 21.7 %fusion.59 = f32[12,64,128,128]{3,2,1,0:T(8,128)} fusion(bf16[40,12,66,130]{3,0,2,1:T(8,128)(2,1)} %scatter.49, bf16[9,128,40]{1,2,0:T(8,128)(2,1)S(1)} %copy-done.5), kind=kOutput, calls=%fused_computation.81 | convolution fusion | flops 1006632960 | bytes 58206208 | tf_op jit(solution)/shard_map/oi,ifrc->ofrc/dot_general | solution.py:86
  695.0 24.0 %fusion.61 = f32[12,64,128,128]{3,2,1,0:T(8,128)} fusion(bf16[40,12,66,130]{3,0,2,1:T(8,128)(2,1)} %scatter.49, bf16[9,128,40]{1,2,0:T(8,128)(2,1)S(1)} %copy-done.5), kind=kOutput, calls=%fused_computation.83 | convolution fusion | flops 1006632960 | bytes 58206208 | tf_op jit(solution)/shard_map/oi,ifrc->ofrc/dot_general | solution.py:86
  719.0 24.0 %fusion.63 = f32[12,64,128,128]{3,2,1,0:T(8,128)} fusion(bf16[40,12,66,130]{3,0,2,1:T(8,128)(2,1)} %scatter.49, bf16[9,128,40]{1,2,0:T(8,128)(2,1)S(1)} %copy-done.5), kind=kOutput, calls=%fused_computation.85 | convolution fusion | flops 1006632960 | bytes 58206208 | tf_op jit(solution)/shard_map/oi,ifrc->ofrc/dot_general | solution.py:86
  743.0 21.9 %fusion.65 = f32[12,64,128,128]{3,2,1,0:T(8,128)} fusion(bf16[40,12,66,130]{3,0,2,1:T(8,128)(2,1)} %scatter.49, bf16[9,128,40]{1,2,0:T(8,128)(2,1)S(1)} %copy-done.5), kind=kOutput, calls=%fused_computation.87 | convolution fusion | flops 1006632960 | bytes 58206208 | tf_op jit(solution)/shard_map/oi,ifrc->ofrc/dot_general | solution.py:86
  764.9 24.0 %fusion.67 = f32[12,64,128,128]{3,2,1,0:T(8,128)} fusion(bf16[40,12,66,130]{3,0,2,1:T(8,128)(2,1)} %scatter.49, bf16[9,128,40]{1,2,0:T(8,128)(2,1)S(1)} %copy-done.5), kind=kOutput, calls=%fused_computation.89 | convolution fusion | flops 1006632960 | bytes 58206208 | tf_op jit(solution)/shard_map/oi,ifrc->ofrc/dot_general | solution.py:86
  788.9 24.0 %fusion.69 = f32[12,64,128,128]{3,2,1,0:T(8,128)} fusion(bf16[40,12,66,130]{3,0,2,1:T(8,128)(2,1)} %scatter.49, bf16[9,128,40]{1,2,0:T(8,128)(2,1)S(1)} %copy-done.5), kind=kOutput, calls=%fused_computation.91 | convolution fusion | flops 1006632960 | bytes 58206208 | tf_op jit(solution)/shard_map/oi,ifrc->ofrc/dot_general | solution.py:86
  812.9 21.6 %fusion.71 = f32[12,64,128,128]{3,2,1,0:T(8,128)} fusion(bf16[40,12,66,130]{3,0,2,1:T(8,128)(2,1)} %scatter.49, bf16[9,128,40]{1,2,0:T(8,128)(2,1)S(1)} %copy-done.5), kind=kOutput, calls=%fused_computation.93 | convolution fusion | flops 1006632960 | bytes 58206208 | tf_op jit(solution)/shard_map/oi,ifrc->ofrc/dot_general | solution.py:86
  834.6 146.5 %fusion.2 = bf16[128,12,64,128]{0,3,2,1:T(8,128)(2,1)} fusion(f32[12,64,128,128]{3,2,1,0:T(8,128)} %fusion.57, f32[12,64,128,128]{3,2,1,0:T(8,128)} %fusion.59, f32[12,64,128,128]{3,2,1,0:T(8,128)} %fusion.61, f32[12,64,128,128]{3,2,1,0:T(8,128)} %fusion.63, f32[12,64,128,128]{3,2,1,0:T(8,128)} %fusion.65, f32[12,64,128,128]{3,2,1,0:T(8,128)} %fusion.67, ...), kind=kOutput, calls=%fused_computation.8 | convolution fusion | flops 1937768448 | bytes 435694080 | tf_op jit(solution)/shard_map/oi,ifrc->ofrc/dot_general | solution.py:86
  1028.2 100.9 %rev.9 = f32[128,48,512]{2,0,1:T(8,128)} reverse(f32[128,48,512]{2,0,1:T(8,128)} %bitcast.335), dimensions={2} | reverse | bytes 25165824 | tf_op jit(solution)/shard_map/jit(_flip)/rev | solution.py:50
  1129.1 14.6 broadcast_select_fusion
  1152.1 223.1 %all-reduce.5 = bf16[128,48,512]{2,0,1:T(8,128)(2,1)} all-reduce(f32[128,48,512]{2,0,1:T(8,128)} %broadcast_select_fusion), channel_id=1, replica_groups=mesh['band'=8,'tile'=4] {'band','tile'}, use_global_device_ids=true, to_apply=%region_6.7 | all-reduce | flops 3145728 | bytes 18874368 | tf_op jit(solution)/shard_map/psum | solution.py:51
  1402.1 19.1 %pad_maximum_fusion = bf16[128,12,66,130]{0,3,2,1:T(8,128)(2,1)S(1)} fusion(bf16[128,12,66,1]{0,3,2,1:T(2,128)(2,1)S(1)} %collective-permute-done.7, bf16[128,12,1,128]{0,3,2,1:T(8,128)(2,1)S(1)} %collective-permute-done.5, bf16[128,12,64,128]{0,3,2,1:T(8,128)(2,1)} %fusion.2, bf16[128,12,1,128]{0,3,2,1:T(8,128)(2,1)S(1)} %collective-permute-done.4, ...), kind=kLoop, calls=%fused_computation.54 | loop fusion | flops 131788800 | bytes 52715520 | tf_op jit(solution)/shard_map/concatenate | solution.py:16
  1431.3 20.7 %scatter.62 = bf16[128,12,66,130]{0,3,2,1:T(8,128)(2,1)} dynamic-update-slice(bf16[128,12,66,130]{0,3,2,1:T(8,128)(2,1)} %copy-done, bf16[128,12,66,1]{0,3,2,1:T(2,128)(2,1)S(1)} %broadcast_select_fusion.3, s32[]{:T(128)} %constant.262.clone.1, s32[]{:T(128)} %constant.262.clone.1, s32[]{:T(128)} %constant.262.clone.1, s32[]{:T(128)} %constant.262.clone.1) | dynamic-update-slice | bytes 405508 | tf_op jit(solution)/shard_map/scatter | solution.py:70
  1454.2 20.7 %scatter.63 = bf16[128,12,66,130]{0,3,2,1:T(8,128)(2,1)} dynamic-update-slice(bf16[128,12,66,130]{0,3,2,1:T(8,128)(2,1)} %scatter.62, bf16[128,12,66,1]{0,3,2,1:T(2,128)(2,1)S(1)} %broadcast_select_fusion.2, s32[]{:T(128)} %constant.262.clone.1, s32[]{:T(128)} %constant.262.clone.1, s32[]{:T(128)} %constant.262.clone.1, s32[]{:T(128)} %constant.278.clone.1) | dynamic-update-slice | bytes 405508 | tf_op jit(solution)/shard_map/scatter | solution.py:71
  1475.0 25.1 %fusion.36 = f32[12,64,128,128]{3,2,1,0:T(8,128)} fusion(bf16[128,12,66,130]{0,3,2,1:T(8,128)(2,1)} %scatter.63, bf16[9,128,128]{2,1,0:T(8,128)(2,1)S(1)} %copy-done.4), kind=kOutput, calls=%fused_computation.55 | convolution fusion | flops 3221225472 | bytes 75530240 | tf_op jit(solution)/shard_map/oi,ifrc->ofrc/dot_general | solution.py:86
  1500.1 25.1 %fusion.38 = f32[12,64,128,128]{3,2,1,0:T(8,128)} fusion(bf16[128,12,66,130]{0,3,2,1:T(8,128)(2,1)} %scatter.63, bf16[9,128,128]{2,1,0:T(8,128)(2,1)S(1)} %copy-done.4), kind=kOutput, calls=%fused_computation.57 | convolution fusion | flops 3221225472 | bytes 75530240 | tf_op jit(solution)/shard_map/oi,ifrc->ofrc/dot_general | solution.py:86
  1525.2 24.7 %fusion.40 = f32[12,64,128,128]{3,2,1,0:T(8,128)} fusion(bf16[128,12,66,130]{0,3,2,1:T(8,128)(2,1)} %scatter.63, bf16[9,128,128]{2,1,0:T(8,128)(2,1)S(1)} %copy-done.4), kind=kOutput, calls=%fused_computation.59 | convolution fusion | flops 3221225472 | bytes 75530240 | tf_op jit(solution)/shard_map/oi,ifrc->ofrc/dot_general | solution.py:86
  1549.9 25.2 %fusion.42 = f32[12,64,128,128]{3,2,1,0:T(8,128)} fusion(bf16[128,12,66,130]{0,3,2,1:T(8,128)(2,1)} %scatter.63, bf16[9,128,128]{2,1,0:T(8,128)(2,1)S(1)} %copy-done.4), kind=kOutput, calls=%fused_computation.61 | convolution fusion | flops 3221225472 | bytes 75530240 | tf_op jit(solution)/shard_map/oi,ifrc->ofrc/dot_general | solution.py:86
  1575.1 25.1 %fusion.44 = f32[12,64,128,128]{3,2,1,0:T(8,128)} fusion(bf16[128,12,66,130]{0,3,2,1:T(8,128)(2,1)} %scatter.63, bf16[9,128,128]{2,1,0:T(8,128)(2,1)S(1)} %copy-done.4), kind=kOutput, calls=%fused_computation.63 | convolution fusion | flops 3221225472 | bytes 75530240 | tf_op jit(solution)/shard_map/oi,ifrc->ofrc/dot_general | solution.py:86
  1600.2 24.7 %fusion.46 = f32[12,64,128,128]{3,2,1,0:T(8,128)} fusion(bf16[128,12,66,130]{0,3,2,1:T(8,128)(2,1)} %scatter.63, bf16[9,128,128]{2,1,0:T(8,128)(2,1)S(1)} %copy-done.4), kind=kOutput, calls=%fused_computation.65 | convolution fusion | flops 3221225472 | bytes 75530240 | tf_op jit(solution)/shard_map/oi,ifrc->ofrc/dot_general | solution.py:86
  1625.0 25.1 %fusion.48 = f32[12,64,128,128]{3,2,1,0:T(8,128)} fusion(bf16[128,12,66,130]{0,3,2,1:T(8,128)(2,1)} %scatter.63, bf16[9,128,128]{2,1,0:T(8,128)(2,1)S(1)} %copy-done.4), kind=kOutput, calls=%fused_computation.67 | convolution fusion | flops 3221225472 | bytes 75530240 | tf_op jit(solution)/shard_map/oi,ifrc->ofrc/dot_general | solution.py:86
  1650.1 25.1 %fusion.50 = f32[12,64,128,128]{3,2,1,0:T(8,128)} fusion(bf16[128,12,66,130]{0,3,2,1:T(8,128)(2,1)} %scatter.63, bf16[9,128,128]{2,1,0:T(8,128)(2,1)S(1)} %copy-done.4), kind=kOutput, calls=%fused_computation.69 | convolution fusion | flops 3221225472 | bytes 75530240 | tf_op jit(solution)/shard_map/oi,ifrc->ofrc/dot_general | solution.py:86
  1675.2 150.0 %fusion.5 = bf16[128,12,64,128]{0,3,2,1:T(8,128)(2,1)} fusion(f32[12,64,128,128]{3,2,1,0:T(8,128)} %fusion.36, f32[12,64,128,128]{3,2,1,0:T(8,128)} %fusion.38, f32[12,64,128,128]{3,2,1,0:T(8,128)} %fusion.40, f32[12,64,128,128]{3,2,1,0:T(8,128)} %fusion.42, f32[12,64,128,128]{3,2,1,0:T(8,128)} %fusion.44, f32[12,64,128,128]{3,2,1,0:T(8,128)} %fusion.46, ...), kind=kOutput, calls=%fused_computation.11 | convolution fusion | flops 4152360960 | bytes 453018112 | tf_op jit(solution)/shard_map/oi,ifrc->ofrc/dot_general | solution.py:86
  1825.2 33.9 %copy.130 = bf16[128,12,64,128]{3,2,1,0:T(8,128)(2,1)} copy(bf16[128,12,64,128]{0,3,2,1:T(8,128)(2,1)} %fusion.5) | data formatting | bytes 50331648 | tf_op jit(solution)/shard_map/convert_element_type | solution.py:92
  (135 shorter events, 280.6 us)
Async XLA Ops:
  0.0 59.2 %copy-start.7 = (s32[12,4,3]{0,1,2:T(4,128)S(1)}, s32[12,4,3]{0,1,2:T(4,128)}, u32[]{:S(2)}) copy-start(s32[12,4,3]{0,1,2:T(4,128)} %param.29) | copy-start | bytes 1732
  5.8 46.8 %all-to-all-start.1 = ((s32[32,1,24]{2,1,0:T(1,128)}), s32[32,1,24]{2,1,0:T(1,128)S(1)}, u32[]{:S(2)}, u32[]{:S(2)}) async-start(s32[32,1,24]{2,1,0:T(1,128)} %bitcast.8), calls=%async_computation.1 | async-start | bytes 32768 | tf_op jit(solution)/shard_map/all_to_all | solution.py:147
  52.6 179.6 %all-to-all-start = ((bf16[32,24,40,128]{3,2,1,0:T(8,128)(2,1)}), bf16[32,24,40,128]{3,2,1,0:T(8,128)(2,1)}, u32[]{:S(2)}, u32[]{:S(2)}) async-start(bf16[32,24,40,128]{3,2,1,0:T(8,128)(2,1)} %bitcast.343), calls=%async_computation | async-start | bytes 15728640 | tf_op jit(solution)/shard_map/all_to_all | solution.py:140
  59.7 253.4 %copy-start.8 = (pred[48]{0:T(512)(128)(4,1)}, pred[48]{0:T(512)(128)(4,1)S(1)}, u32[]{:S(2)}) copy-start(pred[48]{0:T(512)(128)(4,1)S(1)} %eq.89) | copy-start | bytes 148
  59.7 241.5 %copy-start.6 = (s32[1024]{0:T(1024)}, s32[1024]{0:T(1024)S(1)}, u32[]{:S(2)}) copy-start(s32[1024]{0:T(1024)S(1)} %pad_clamp_fusion) | copy-start | bytes 12292
  295.2 0.9 copy-start.2
  413.2 11.1 collective-permute-start
  414.5 9.8 collective-permute-start.1
  443.0 21.4 %collective-permute-start.2 = (bf16[40,12,66,1]{2,0,3,1:T(8,128)(2,1)S(1)}, bf16[40,12,66,1]{2,0,3,1:T(8,128)(2,1)S(1)}, u32[]{:S(2)}, u32[]{:S(2)}) collective-permute-start(bf16[40,12,66,1]{2,0,3,1:T(8,128)(2,1)S(1)} %copy.113), channel_id=1, source_target_pairs={{0,1},{1,2},{2,3},{4,5},{5,6},{6,7},{8,9},{9,10},{10,11},{12,13},{... | collective-permute-start | bytes 190088 | tf_op jit(solution)/shard_map/ppermute | solution.py:14
  455.0 15.6 collective-permute-start.3
  495.3 5.6 copy-start.1
  504.7 144.6 %copy-start.5 = (bf16[9,128,40]{1,2,0:T(8,128)(2,1)S(1)}, bf16[9,128,40]{1,2,0:T(8,128)(2,1)}, u32[]{:S(2)}) copy-start(bf16[9,128,40]{1,2,0:T(8,128)(2,1)} %param.30) | copy-start | bytes 276484
  812.9 21.7 %copy-start.10 = (f32[128]{0:T(128)S(1)}, f32[128]{0:T(128)}, u32[]{:S(2)}) copy-start(f32[128]{0:T(128)} %param.31) | copy-start | bytes 1540
  1006.6 122.5 %copy-start.9 = (pred[48]{0:T(512)(128)(4,1)S(1)}, pred[48]{0:T(512)(128)(4,1)}, u32[]{:S(2)}) copy-start(pred[48]{0:T(512)(128)(4,1)} %copy-done.8) | copy-start | bytes 148
  1028.2 115.6 %copy-start.3 = (bf16[128,12,1,128]{0,3,2,1:T(8,128)(2,1)S(1)}, bf16[128,12,1,128]{0,3,2,1:T(8,128)(2,1)}, u32[]{:S(2)}) copy-start(bf16[128,12,1,128]{0,3,2,1:T(8,128)(2,1)} %get-tuple-element.107) | copy-start | bytes 1179652
  1143.8 243.7 %collective-permute-start.4 = (bf16[128,12,1,128]{0,3,2,1:T(8,128)(2,1)S(1)}, bf16[128,12,1,128]{0,3,2,1:T(8,128)(2,1)S(1)}, u32[]{:S(2)}, u32[]{:S(2)}) collective-permute-start(bf16[128,12,1,128]{0,3,2,1:T(8,128)(2,1)S(1)} %copy-done.3), channel_id=1, source_target_pairs={{0,4},{4,8},{8,12},{12,16},{16,20},{20,24},{24,28},{1,5},{5,9},{9,... | collective-permute-start | bytes 1179656 | tf_op jit(solution)/shard_map/ppermute | solution.py:14
  1150.8 236.7 %collective-permute-start.5 = (bf16[128,12,1,128]{0,3,2,1:T(8,128)(2,1)S(1)}, bf16[128,12,1,128]{0,3,2,1:T(8,128)(2,1)S(1)}, u32[]{:S(2)}, u32[]{:S(2)}) collective-permute-start(bf16[128,12,1,128]{0,3,2,1:T(8,128)(2,1)S(1)} %get-tuple-element.108), channel_id=1, source_target_pairs={{4,0},{8,4},{12,8},{16,12},{20,16},{24,20},{28,24},{5,1},{9,5},{13... | collective-permute-start | bytes 1179656 | tf_op jit(solution)/shard_map/ppermute | solution.py:15
  1390.1 84.9 %copy-start.4 = (bf16[9,128,128]{2,1,0:T(8,128)(2,1)S(1)}, bf16[9,128,128]{2,1,0:T(8,128)(2,1)}, u32[]{:S(2)}) copy-start(bf16[9,128,128]{2,1,0:T(8,128)(2,1)} %param.32) | copy-start | bytes 884740
  1390.1 7.6 collective-permute-start.6
  1392.8 9.2 collective-permute-start.7
  1421.7 9.1 copy-start
  1650.1 25.1 %copy-start.11 = (f32[128]{0:T(128)S(1)}, f32[128]{0:T(128)}, u32[]{:S(2)}) copy-start(f32[128]{0:T(128)} %param.33) | copy-start | bytes 1540
where the time goes:
time: 1880 us; the launch traced here: 1860 us
  matrix products  699 us (37%)
  local copies, waits for them, and re-layouts  527 us (28%)
  blocking collectives  318 us (17%)
  waiting for transfers between devices  178 us (9%)
  other arithmetic  101 us (5%)
  starting transfers between devices  36.1 us (2%)
    dot_general x18, matrix products, conv_layer(): jnp.einsum('oi,ifrc->ofrc', weight[3 * row_off + col_off], window, prefer...  682 us
    psum x2, blocking collectives, seam_fill(): seam_lines = lax.psum(chosen, ('band', 'tile')).astype(jnp.bfloat16)  318 us
    all_to_all x1, waiting for transfers between devices, local(): lax.all_to_all(outgoing.reshape(devices, capacity, fields, block_len), ('...  171 us
    scatter x2, local copies, waits for them, and re-layouts, seam_fill(): padded.at[:, :, :, -1]  108 us
    rev x2, local copies, waits for them, and re-layouts, seam_fill(): chosen = jnp.where(reverse, jnp.flip(chosen, axis=2), chosen)  108 us
    scatter x2, local copies, waits for them, and re-layouts, seam_fill(): padded.at[:, :, :, 0]  69.7 us
    concatenate x3, other arithmetic, with_halo(): shard = jnp.concatenate([before, shard, after], axis=dim)  41.7 us
  transfers between devices with their start and end apart: 10, of which 3 were waited for; matrix products, arithmetic and copies ran while one was open for 4% of the time, Pallas kernels for 0%

commit v1 on v0

v1 whole, which is shorter than its diff:
```python
import functools

import jax
import jax.numpy as jnp
from jax import lax
from jax.experimental import pallas as pl
from jax.experimental.pallas import tpu as pltpu
from jax.sharding import PartitionSpec as P

BF = jnp.bfloat16
F32 = jnp.float32
VMEM_LIMIT = 60 * 1024 * 1024
PAIRS = 8
GELU_COEF = (
    0.7978842684146765,
    0.03633414911622174,
    -3.30267008968913e-05,
    -5.527338755532785e-05,
    3.974071022505988e-06,
    -1.3378322650770525e-07,
    1.8139281733930472e-09,
)
GELU_CAP = 30.0


def gelu(v):
    u = jnp.minimum(v * v, GELU_CAP)
    q = jnp.full_like(u, GELU_COEF[-1])
    for c in GELU_COEF[-2::-1]:
        q = q * u + c
    half = 0.5 * v
    return half + half * jnp.tanh(v * q)


def partial_kernel(pos_ref, src_ref, w_ref, out_ref):
    s = pl.program_id(0)
    per_step = w_ref.shape[0]
    top, blk = w_ref.shape[1], w_ref.shape[2]

    @pl.when(s == 0)
    def _():
        out_ref[...] = jnp.zeros_like(out_ref)

    for j in range(per_step):
        x = src_ref[:, j * blk : (j + 1) * blk]
        for k in range(top):
            y = jnp.dot(x, w_ref[j, k], preferred_element_type=F32).astype(BF)
            out_ref[pos_ref[(s * per_step + j) * top + k]] = y


def partials(position, source, weights, slots):
    fields = source.shape[0]
    src_count, top, blk, _ = weights.shape
    step = 4
    return pl.pallas_call(
        partial_kernel,
        out_shape=jax.ShapeDtypeStruct((slots, fields, blk), BF),
        grid_spec=pltpu.PrefetchScalarGridSpec(
            num_scalar_prefetch=1,
            grid=(src_count // step,),
            in_specs=[
                pl.BlockSpec((fields, step * blk), lambda i, p: (0, i)),
                pl.BlockSpec((step, top, blk, blk), lambda i, p: (i, 0, 0, 0)),
            ],
            out_specs=pl.BlockSpec((slots, fields, blk), lambda i, p: (0, 0, 0)),
        ),
        compiler_params=pltpu.CompilerParams(vmem_limit_bytes=VMEM_LIMIT),
        name="partials",
    )(position, source, weights)


def collect_kernel(slot_ref, arr_ref, out_ref, acc_ref):
    i = pl.program_id(0)
    n = arr_ref.shape[0]

    @pl.when(i == 0)
    def _():
        acc_ref[...] = jnp.zeros_like(acc_ref)

    def body(j, _):
        slot = slot_ref[i * n + j]
        acc_ref[slot] = acc_ref[slot] + arr_ref[j].astype(F32)
        return 0

    lax.fori_loop(0, n, body, 0, unroll=4)

    @pl.when(i == pl.num_programs(0) - 1)
    def _():
        out_ref[...] = acc_ref[: out_ref.shape[0]].astype(BF)


def collect(slots, arrived, slots_dev):
    count, fields, blk = arrived.shape
    steps = 8
    return pl.pallas_call(
        collect_kernel,
        out_shape=jax.ShapeDtypeStruct((slots_dev, fields, blk), BF),
        grid_spec=pltpu.PrefetchScalarGridSpec(
            num_scalar_prefetch=1,
            grid=(steps,),
            in_specs=[pl.BlockSpec((count // steps, fields, blk), lambda i, p: (i, 0, 0))],
            out_specs=pl.BlockSpec((slots_dev, fields, blk), lambda i, p: (0, 0, 0)),
            scratch_shapes=[pltpu.VMEM((slots_dev + 1, fields, blk), F32)],
        ),
        compiler_params=pltpu.CompilerParams(vmem_limit_bytes=VMEM_LIMIT),
        name="collect",
    )(slots, arrived)


def conv_kernel(
    first, x_ref, top_ref, bot_ref, left_ref, right_ref, wa_ref, wb_ref, b_ref, out_ref, *scratch
):
    sl, win = scratch[0], scratch[1]
    rows = out_ref.shape[0] if first else out_ref.shape[2]
    cols = sl.shape[1]
    width = sl.shape[2] // 2
    chan = left_ref.shape[-1]

    def put(pair, parity, row32, lo, hi):
        win[parity, 8 : 8 + cols, :] = row32
        win[parity, 7:8, :] = lo
        win[parity, 8 + cols : 9 + cols, :] = hi
        before = win[parity, 7 : 7 + cols, :]
        after = win[parity, 9 : 9 + cols, :]
        base = parity * width
        if first:
            g = before + pltpu.roll(row32, chan, 1) + pltpu.roll(after, 2 * chan, 1)
            sl[pair, :, base : base + width] = g.astype(BF)
        else:
            sl[pair, :, base : base + cols] = before.astype(BF)
            sl[pair, :, base + cols : base + 2 * cols] = row32.astype(BF)
            sl[pair, :, base + 2 * cols : base + 3 * cols] = after.astype(BF)

    def wide(v):
        if first:
            v = jnp.concatenate([v, jnp.zeros((v.shape[0], cols - chan), v.dtype)], axis=1)
        return v

    def row_at(r):
        if first:
            y = x_ref[r].astype(F32)
            y = jnp.concatenate([y, jnp.zeros((cols - chan, cols), F32)], axis=0)
            return y.T
        return x_ref[r].astype(F32)

    def halo_row(ref):
        full = wide(ref[0].astype(F32))
        return full[:cols], full[cols : cols + 1], full[cols + 1 : cols + 2]

    row, lo, hi = halo_row(top_ref)
    put(0, 0, row, lo, hi)
    row, lo, hi = halo_row(bot_ref)
    put(rows // 2, 1, row, lo, hi)

    def fill(i, _):
        for parity in range(2):
            r = 2 * i + parity
            put(
                i + parity,
                1 - parity,
                row_at(r),
                wide(left_ref[0, pl.ds(r, 1), :]),
                wide(right_ref[0, pl.ds(r, 1), :]),
            )
        return 0

    lax.fori_loop(0, rows // 2, fill, 0, unroll=2)

    def chunk(g, _):
        p0 = g * PAIRS
        a = sl[pl.ds(p0, PAIRS)].reshape(PAIRS * cols, 2 * width)
        b = sl[pl.ds(p0 + 1, PAIRS)].reshape(PAIRS * cols, 2 * width)
        y = jnp.dot(a, wa_ref[...], preferred_element_type=F32) + jnp.dot(
            b, wb_ref[...], preferred_element_type=F32
        )
        hid = y.shape[1] // 2
        if first:
            y = gelu(y + b_ref[...]).astype(BF)
            for p in range(PAIRS):
                for q in range(2):
                    out_ref[2 * (p0 + p) + q] = y[p * cols : (p + 1) * cols, q * hid : (q + 1) * hid]
        else:
            flip = scratch[2]
            n = 2 * PAIRS
            for p in range(PAIRS):
                for q in range(2):
                    part = y[p * cols : (p + 1) * cols, q * hid : (q + 1) * hid]
                    flip[pl.ds(2 * p + q, hid, stride=n), :] = part.T

            def finish(o, _):
                for j in range(8):
                    oo = o * 8 + j
                    v = flip[pl.ds(oo * n, n), :]
                    out_ref[oo, 0, pl.ds(g * n, n), :] = gelu(v + b_ref[oo]).astype(BF)
                return 0

            lax.fori_loop(0, hid // 8, finish, 0)
        return 0

    lax.fori_loop(0, rows // (2 * PAIRS), chunk, 0)


def conv(first, x, halos, weight, bias, face_count, rows, out_cols):
    top, bot, left, right = halos
    hid, chan = weight.shape[1], weight.shape[2]
    cols = out_cols
    w = weight.reshape(3, 3, hid, chan).transpose(0, 1, 3, 2)
    if first:
        w = w.reshape(3, 3 * chan, hid)
        w = jnp.pad(w, ((0, 0), (0, cols - 3 * chan), (0, 0)))
    else:
        w = w.reshape(3, 3 * chan, hid)
    width = w.shape[1]
    zero = jnp.zeros((width, hid), w.dtype)
    wide = [
        jnp.concatenate([w[a] if a < 3 else zero, w[a - 1] if a > 0 else zero], axis=1)
        for a in range(4)
    ]
    wa = jnp.concatenate(wide[:2], axis=0)
    wb = jnp.concatenate(wide[2:], axis=0)
    scratch = [
        pltpu.VMEM((rows // 2 + 1, cols, 2 * width), BF),
        pltpu.VMEM((2, cols + 16, cols), F32),
    ]
    if first:
        bias_in = jnp.concatenate([bias, bias])[None, :]
        bias_spec = pl.BlockSpec((1, 2 * hid), lambda f: (0, 0))
        out_shape = jax.ShapeDtypeStruct((face_count * rows, cols, hid), BF)
        out_spec = pl.BlockSpec((rows, cols, hid), lambda f: (f, 0, 0))
    else:
        bias_in = bias
        bias_spec = pl.BlockSpec(memory_space=pltpu.SMEM)
        out_shape = jax.ShapeDtypeStruct((hid, face_count, rows, cols), BF)
        out_spec = pl.BlockSpec((hid, 1, rows, cols), lambda f: (0, f, 0, 0))
        scratch.append(pltpu.VMEM((hid * 2 * PAIRS, cols), F32))
    return pl.pallas_call(
        functools.partial(conv_kernel, first),
        out_shape=out_shape,
        grid=(face_count,),
        in_specs=[
            pl.BlockSpec((rows,) + x.shape[1:], lambda f: (f, 0, 0)),
            pl.BlockSpec((1,) + top.shape[1:], lambda f: (f, 0, 0)),
            pl.BlockSpec((1,) + bot.shape[1:], lambda f: (f, 0, 0)),
            pl.BlockSpec((1,) + left.shape[1:], lambda f: (f, 0, 0)),
            pl.BlockSpec((1,) + right.shape[1:], lambda f: (f, 0, 0)),
            pl.BlockSpec(wa.shape, lambda f: (0, 0)),
            pl.BlockSpec(wb.shape, lambda f: (0, 0)),
            bias_spec,
        ],
        out_specs=out_spec,
        scratch_shapes=scratch,
        compiler_params=pltpu.CompilerParams(vmem_limit_bytes=VMEM_LIMIT),
        name="conv1" if first else "conv2",
    )(x, top, bot, left, right, wa, wb, bias_in)


def halos_of(top, bottom, left, right, seam_table):
    faces, cols, chan = top.shape
    rows = left.shape[1]
    nb, nt = lax.axis_size("band"), lax.axis_size("tile")
    band, tile = lax.axis_index("band"), lax.axis_index("tile")
    side = cols * nt

    row_edge = jnp.where(band == 0, top, bottom).reshape(nb, faces * cols // nb, chan)
    col_edge = jnp.where(tile == 0, left, right).reshape(nt, faces * rows // nt, chan)
    row_part = lax.all_to_all(row_edge, "band", 0, 0, tiled=True)
    col_part = lax.all_to_all(col_edge, "tile", 0, 0, tiled=True)
    mine = jnp.concatenate([row_part[0], row_part[-1], col_part[0], col_part[-1]], axis=0)
    rp, cp = row_edge.shape[1], col_edge.shape[1]
    every = lax.all_gather(mine, ("band", "tile"), axis=0, tiled=False)
    every = every.reshape(nb, nt, 2 * rp + 2 * cp, chan)
    row_all = every[:, :, : 2 * rp].reshape(nb, nt, 2, rp, chan)
    row_all = row_all.transpose(2, 0, 3, 1, 4).reshape(2, faces, cols, nt, chan)
    row_all = row_all.transpose(1, 0, 3, 2, 4).reshape(faces, 2, side, chan)
    col_all = every[:, :, 2 * rp :].reshape(nb, nt, 2, cp, chan)
    col_all = col_all.transpose(2, 1, 3, 0, 4).reshape(2, faces, rows, nb, chan)
    col_all = col_all.transpose(1, 0, 3, 2, 4).reshape(faces, 2, side, chan)
    lines = jnp.concatenate([row_all, col_all], axis=1).reshape(faces * 4, side, chan)
    lines = jnp.pad(lines, ((0, 0), (1, 1), (0, 0)))

    def segments(which, start, length):
        index = seam_table[:, which, 0] * 4 + seam_table[:, which, 1]
        rev = seam_table[:, which, 2] == 1
        first = jnp.where(rev, side - start - length, start)
        got = jax.vmap(
            lambda i, s: lax.dynamic_slice(lines, (i, s, 0), (1, length + 2, chan))[0]
        )(index, first)
        flip = jnp.eye(length + 2, dtype=BF)[::-1]
        flipped = jnp.einsum("pq,fqc->fpc", flip, got, preferred_element_type=F32).astype(BF)
        return jnp.where(rev[:, None, None], flipped, got)

    def shift(x, axis, size, forward):
        pairs = [(i, i + 1) if forward else (i + 1, i) for i in range(size - 1)]
        return lax.ppermute(x, axis, pairs)

    above = shift(bottom, "band", nb, True)
    below = shift(top, "band", nb, False)
    ext_left = jnp.concatenate([above[:, :1], left, below[:, :1]], axis=1)
    ext_right = jnp.concatenate([above[:, -1:], right, below[:, -1:]], axis=1)
    from_left = shift(ext_right, "tile", nt, True)
    from_right = shift(ext_left, "tile", nt, False)
    lefts = jnp.where(tile == 0, segments(2, band * rows, rows), from_left)
    rights = jnp.where(tile == nt - 1, segments(3, band * rows, rows), from_right)

    def line(at_edge, seam, inner, at):
        seam = jnp.concatenate([seam[:, 1:-1], seam[:, :1], seam[:, -1:]], axis=1)
        inner = jnp.concatenate([inner, lefts[:, at : at + 1], rights[:, at : at + 1]], axis=1)
        return jnp.where(at_edge, seam, inner)

    tops = line(band == 0, segments(0, tile * cols, cols), above, 0)
    bots = line(band == nb - 1, segments(1, tile * cols, cols), below, rows + 1)
    return tops, bots, lefts[:, 1:-1].astype(F32), rights[:, 1:-1].astype(F32)


def local(
    source,
    regrid_weights,
    dest_group,
    dest_block,
    seam_table,
    conv1_weight,
    conv1_bias,
    conv2_weight,
    conv2_bias,
):
    fields = source.shape[0]
    src_count, top_count, block_len, _ = regrid_weights.shape
    nb, nt = lax.axis_size("band"), lax.axis_size("tile")
    devices = nb * nt
    capacity = 3 * src_count * top_count // devices
    rows = block_len * nt // nb
    faces = seam_table.shape[0]
    slots_dev = faces * rows
    items = src_count * top_count
    target_dev = dest_group.reshape(items)
    target_slot = dest_block.reshape(items)
    onehot = (target_dev[:, None] == jnp.arange(devices, dtype=jnp.int32)[None, :]).astype(F32)
    earlier = (jnp.arange(items)[:, None] > jnp.arange(items)[None, :]).astype(BF)
    before = jnp.dot(earlier, onehot.astype(BF), preferred_element_type=F32)
    rank_in = jnp.sum(before * onehot, axis=1).astype(jnp.int32)
    position = target_dev * capacity + rank_in
    hit = position[None, :] == jnp.arange(devices * capacity, dtype=jnp.int32)[:, None]
    out_slots = slots_dev + jnp.sum(jnp.where(hit, target_slot[None, :] - slots_dev, 0), axis=1)
    outgoing = partials(position, source, regrid_weights, devices * capacity)
    axes = ("band", "tile")
    arrived = lax.all_to_all(
        outgoing.reshape(devices, capacity, fields, block_len), axes, 0, 0, tiled=True
    )
    arrived_slots = lax.all_to_all(
        out_slots.reshape(devices, capacity), axes, 0, 0, tiled=True
    )
    grid = collect(
        arrived_slots.reshape(-1), arrived.reshape(devices * capacity, fields, block_len), slots_dev
    )
    tiles = grid.reshape(faces, rows, fields, block_len)
    halos = halos_of(
        tiles[:, 0].transpose(0, 2, 1),
        tiles[:, -1].transpose(0, 2, 1),
        tiles[:, :, :, 0],
        tiles[:, :, :, -1],
        seam_table,
    )
    hidden = conv(True, grid, halos, conv1_weight, conv1_bias, faces, rows, block_len)
    tiles = hidden.reshape(faces, rows, block_len, hidden.shape[2])
    halos = halos_of(
        tiles[:, 0], tiles[:, -1], tiles[:, :, 0], tiles[:, :, -1], seam_table
    )
    return conv(False, hidden, halos, conv2_weight, conv2_bias, faces, rows, block_len)


def solution(mesh):
    return jax.shard_map(
        local,
        mesh=mesh,
        in_specs=(
            P(None, ("band", "tile")),
            P(("band", "tile"), None, None, None),
            P(("band", "tile"), None),
            P(("band", "tile"), None),
            P(),
            P(),
            P(),
            P(),
            P(),
        ),
        out_specs=P(None, None, "band", "tile"),
        check_vma=False,
    )
```

time: 1880 us -> 802 us (0.43)
  matrix products: 699 us -> 2.31 us
  local copies, waits for them, and re-layouts: 527 us -> 152 us
  blocking collectives: 318 us -> 0 us
  Pallas kernels: 0 us -> 249 us
  waiting for transfers between devices: 178 us -> 292 us
  other arithmetic: 101 us -> 27.9 us
  starting transfers between devices: 36.1 us -> 55.6 us
    dot_general x20 -> x9, matrix products: 699 us -> 2.31 us  [the longest x8 2.1 us: segments(): jnp.einsum('pq,fqc->fpc', flip, got, preferred_element_type=F32).astype(BF)]
    psum x2 -> x0, blocking collectives: 318 us -> none  [seam_fill(): seam_lines = lax.psum(chosen, ('band', 'tile')).astype(jnp.bfloat16)]
    pallas_call x0 -> x4, Pallas kernels: none -> 249 us  [the longest x2 219 us: conv(): pl.pallas_call(functools.partial(conv_kernel, first), out_shape=out_shape...]
    scatter x6 -> x0, local copies, waits for them, and re-layouts: 209 us -> none  [the longest x2 108 us: seam_fill(): padded.at[:, :, :, -1]]
    rev x2, local copies, waits for them, and re-layouts: 108 us -> 0.33 us  [segments(): flip = jnp.eye(length + 2, dtype=BF)[::-1]]
    all_gather x0 -> x2, waiting for transfers between devices: none -> 78 us  [halos_of(): every = lax.all_gather(mine, ('band', 'tile'), axis=0, tiled=False)]
    convert_element_type x3 -> x4, local copies, waits for them, and re-layouts: 53.1 us -> 0.91 us  [segments(): jnp.einsum('pq,fqc->fpc', flip, got, preferred_element_type=F32).astype(BF)]
    pallas_call x0 -> x2, local copies, waits for them, and re-layouts: none -> 51.8 us  [the longest x1 33.9 us: collect(): pl.pallas_call(collect_kernel, out_shape=jax.ShapeDtypeStruct((slots_dev,...]
  transfers between devices with their start and end apart: 10 -> 16, of which waited for: 3 -> 9; matrix products, arithmetic and copies ran while one was open for 4% -> 13% of each run, Pallas kernels for 0% -> 2%
where the time goes in v1:
time: 802 us; the launch traced here: 793 us
  waiting for transfers between devices  292 us (36%)
  Pallas kernels  249 us (31%)
  local copies, waits for them, and re-layouts  152 us (19%)
  starting transfers between devices  55.6 us (7%)
  other arithmetic  27.9 us (3%)
  between operations  14.4 us (2%)
    pallas_call x2, Pallas kernels, conv(): pl.pallas_call(functools.partial(conv_kernel, first), out_shape=out_shape...  219 us
    all_to_all x1, waiting for transfers between devices, local(): lax.all_to_all(outgoing.reshape(devices, capacity, fields, block_len), ax...  171 us
    all_gather x2, waiting for transfers between devices, halos_of(): every = lax.all_gather(mine, ('band', 'tile'), axis=0, tiled=False)  78 us
    pallas_call x1, local copies, waits for them, and re-layouts, collect(): pl.pallas_call(collect_kernel, out_shape=jax.ShapeDtypeStruct((slots_dev,...  33.9 us
    ppermute x8, starting transfers between devices, shift(): return lax.ppermute(x, axis, pairs)  24.7 us
    ppermute x8, waiting for transfers between devices, shift(): return lax.ppermute(x, axis, pairs)  23.8 us
    gather x8, local copies, waits for them, and re-layouts, segments(): lax.dynamic_slice(lines, (i, s, 0), (1, length + 2, chan))[0]  19.8 us
    pallas_call x1, local copies, waits for them, and re-layouts, conv(): pl.pallas_call(functools.partial(conv_kernel, first), out_shape=out_shape...  17.9 us
  transfers between devices with their start and end apart: 16, of which 9 were waited for; matrix products, arithmetic and copies ran while one was open for 13% of the time, Pallas kernels for 2%

profile of v1, /device:TPU:1, one launch (start us, length us, event | category | flops | bytes accessed | tf_op | source)
XLA Modules:
  0.0 793.5 jit_solution(8822177635050345433)
XLA Ops:
  9.4 7.1 all-to-all-start
  16.5 16.2 %partials.1 = bf16[768,40,128]{2,1,0:T(8,128)(2,1)} custom-call(s32[256]{0:T(256)} %copy-done.12, bf16[40,8192]{1,0:T(8,128)(2,1)} %src_ref.1, bf16[64,4,128,128]{3,2,1,0:T(8,128)(2,1)} %w_ref.1), custom_call_target="tpu_custom_call" | custom-call | tf_op jit(solution)/shard_map/partials/pallas_call | solution.py:55
  32.8 5.9 all-to-all-start.1
  40.7 171.1 %all-to-all-done.1 = bf16[32,24,40,128]{3,2,1,0:T(8,128)(2,1)} async-done(((bf16[32,24,40,128]{3,2,1,0:T(8,128)(2,1)}), bf16[32,24,40,128]{3,2,1,0:T(8,128)(2,1)}, u32[]{:S(2)}, u32[]{:S(2)}) %all-to-all-start.1) | async-done | bytes 7864352 | tf_op jit(solution)/shard_map/all_to_all | solution.py:346
  211.8 13.5 %collect.1.x_ref = bf16[768,40,128]{2,1,0:T(8,128)(2,1)} custom-call(s32[768]{0:T(1024)} %reshape.373.slot_ref, bf16[768,40,128]{2,1,0:T(8,128)(2,1)} %bitcast.2.arr_ref), custom_call_target="tpu_custom_call" | custom-call | tf_op jit(solution)/shard_map/collect/pallas_call | solution.py:95
  225.3 33.9 %copy.274 = bf16[768,40,128]{1,0,2:T(8,128)(2,1)} copy(bf16[768,40,128]{2,1,0:T(8,128)(2,1)} %collect.1.x_ref) | data formatting | bytes 15728640 | tf_op jit(solution)/shard_map/collect/pallas_call | solution.py:95
  259.2 4.2 fusion.70
  265.2 4.4 all-to-all-start.3
  272.9 6.5 all-to-all-start.2
  279.5 6.5 all-to-all-done.2
  291.4 3.3 collective-permute-done
  294.7 6.3 collective-permute-done.1
  301.8 8.3 %collective-permute-start.2 = (bf16[12,66,40]{2,1,0:T(8,128)(2,1)}, bf16[12,66,40]{2,1,0:T(8,128)(2,1)}, u32[]{:S(2)}, u32[]{:S(2)}) collective-permute-start(bf16[12,66,40]{2,1,0:T(8,128)(2,1)} %pad_maximum_fusion.2), channel_id=1, source_target_pairs={{0,1},{1,2},{2,3},{4,5},{5,6},{6,7},{8,9},{9,10},{10,11},{12,13},{... | collective-permute-start | bytes 190088 | tf_op jit(solution)/shard_map/ppermute | solution.py:294
  313.1 32.4 %all-gather.5.cloned.1.call-done = bf16[24576,40]{0,1:T(8,128)(2,1)} async-done(((bf16[768,40]{0,1:T(8,128)(2,1)}), bf16[24576,40]{0,1:T(8,128)(2,1)}) %all-gather.5.cloned.1.call-update) | async-done | bytes 1966096 | tf_op jit(solution)/shard_map/all_gather | solution.py:270
  345.4 4.2 reshape.378
  359.8 3.9 reshape.384
  370.5 8.5 %copy.288 = bf16[12,4,512,40]{3,1,0,2:T(4,128)(2,1)} copy(bf16[12,4,512,40]{2,3,1,0:T(8,128)(2,1)S(1)} %pad_maximum_fusion.1) | data formatting | bytes 3932160 | tf_op jit(solution)/shard_map/concatenate | solution.py:278
  379.0 6.7 pad.16
  403.3 99.4 %conv1.1.x_ref = bf16[768,128,128]{2,1,0:T(8,128)(2,1)} custom-call(bf16[768,40,128]{2,1,0:T(8,128)(2,1)} %collect.1.x_ref, bf16[12,130,40]{2,1,0:T(8,128)(2,1)} %get-tuple-element.73.top_ref, bf16[12,130,40]{2,1,0:T(8,128)(2,1)} %get-tuple-element.74.bot_ref, f32[12,64,40]{2,1,0:T(8,128)} %slice_convert_fusion.3.left_ref, ...), custom_call_target="tpu_custom_call" | custom-call | tf_op jit(solution)/shard_map/conv1/pallas_call | solution.py:236
  502.7 17.9 %copy.301 = bf16[768,128,128]{2,0,1:T(8,128)(2,1)S(1)} copy(bf16[768,128,128]{2,1,0:T(8,128)(2,1)} %conv1.1.x_ref) | data formatting | bytes 50331648 | tf_op jit(solution)/shard_map/conv1/pallas_call | solution.py:236
  520.6 8.9 %copy-done = bf16[768,128,128]{2,0,1:T(8,128)(2,1)} copy-done((bf16[768,128,128]{2,0,1:T(8,128)(2,1)}, bf16[768,128,128]{2,0,1:T(8,128)(2,1)S(1)}, u32[]{:S(2)}) %copy-start) | copy-done | bytes 25165848
  530.3 3.4 all-to-all-start.5
  533.6 3.9 fusion.69
  538.4 3.6 all-to-all-start.4
  542.1 11.2 %all-to-all-done.4 = bf16[8,192,128]{2,1,0:T(8,128)(2,1)S(1)} async-done(((bf16[8,192,128]{2,1,0:T(8,128)(2,1)}), bf16[8,192,128]{2,1,0:T(8,128)(2,1)S(1)}, u32[]{:S(2)}, u32[]{:S(2)}) %all-to-all-start.4) | async-done | bytes 393248 | tf_op jit(solution)/shard_map/all_to_all | solution.py:266
  559.9 14.3 %collective-permute-done.4 = bf16[12,128,128]{2,1,0:T(8,128)(2,1)S(1)} collective-permute-done((bf16[12,128,128]{2,1,0:T(8,128)(2,1)S(1)}, bf16[12,128,128]{2,1,0:T(8,128)(2,1)S(1)}, u32[]{:S(2)}, u32[]{:S(2)}) %collective-permute-start.4) | collective-permute-done | bytes 393248 | tf_op jit(solution)/shard_map/ppermute | solution.py:294
  575.2 4.8 collective-permute-start.6
  582.9 45.6 %all-gather.7.cloned.1.call-done = bf16[24576,128]{1,0:T(8,128)(2,1)} async-done(((bf16[768,128]{1,0:T(8,128)(2,1)}), bf16[24576,128]{1,0:T(8,128)(2,1)}) %all-gather.7.cloned.1.call-update) | async-done | bytes 6291472 | tf_op jit(solution)/shard_map/all_gather | solution.py:270
  628.5 3.3 fusion.71
  635.9 7.5 copy.307
  643.4 6.6 pad.18
  666.8 119.7 %conv2.1 = bf16[128,12,64,128]{3,2,1,0:T(8,128)(2,1)} custom-call(bf16[768,128,128]{2,1,0:T(8,128)(2,1)} %conv1.1.x_ref, bf16[12,130,128]{2,1,0:T(8,128)(2,1)} %maximum_select_fusion.2.top_ref, bf16[12,130,128]{2,1,0:T(8,128)(2,1)} %maximum_select_fusion.3.bot_ref, f32[12,64,128]{2,1,0:T(8,128)} %slice_convert_fusion.1.left_ref, ...), custom_call_target="tpu_custom_call" | custom-call | tf_op jit(solution)/shard_map/conv2/pallas_call | solution.py:236
  (155 shorter events, 86.2 us)
Async XLA Ops:
  7.6 8.9 %copy-start.12 = (s32[256]{0:T(256)}, s32[256]{0:T(256)S(1)}, u32[]{:S(2)}) copy-start(s32[256]{0:T(256)S(1)} %convert_add_fusion.pos_ref) | copy-start | bytes 3076
  9.4 23.3 %all-to-all-start = ((s32[32,1,24]{2,1,0:T(1,128)}), s32[32,1,24]{2,1,0:T(1,128)S(1)}, u32[]{:S(2)}, u32[]{:S(2)}) async-start(s32[32,1,24]{2,1,0:T(1,128)} %bitcast), calls=%async_computation | async-start | bytes 32768 | tf_op jit(solution)/shard_map/all_to_all | solution.py:349
  32.8 179.0 %all-to-all-start.1 = ((bf16[32,24,40,128]{3,2,1,0:T(8,128)(2,1)}), bf16[32,24,40,128]{3,2,1,0:T(8,128)(2,1)}, u32[]{:S(2)}, u32[]{:S(2)}) async-start(bf16[32,24,40,128]{3,2,1,0:T(8,128)(2,1)} %bitcast.237), calls=%async_computation.1 | async-start | bytes 15728640 | tf_op jit(solution)/shard_map/all_to_all | solution.py:346
  259.2 27.5 %copy-start.10 = (bf16[9,128,40]{1,2,0:T(8,128)(2,1)S(1)}, bf16[9,128,40]{1,2,0:T(8,128)(2,1)}, u32[]{:S(2)}) copy-start(bf16[9,128,40]{1,2,0:T(8,128)(2,1)} %param.14) | copy-start | bytes 276484
  259.2 27.5 %copy-start.11 = (s32[12,4,3]{0,1,2:T(4,128)S(1)}, s32[12,4,3]{0,1,2:T(4,128)}, u32[]{:S(2)}) copy-start(s32[12,4,3]{0,1,2:T(4,128)} %param.13) | copy-start | bytes 1732
  259.2 29.3 %copy-start.13 = (f32[128]{0:T(128)S(1)}, f32[128]{0:T(128)}, u32[]{:S(2)}) copy-start(f32[128]{0:T(128)} %param.15) | copy-start | bytes 1540
  265.2 7.7 all-to-all-start.3
  272.9 13.1 %all-to-all-start.2 = ((bf16[8,192,40]{1,2,0:T(8,128)(2,1)}), bf16[8,192,40]{1,2,0:T(8,128)(2,1)S(1)}, u32[]{:S(2)}, u32[]{:S(2)}) async-start(bf16[8,192,40]{1,2,0:T(8,128)(2,1)} %copy.280), calls=%async_computation.2 | async-start | bytes 327680 | tf_op jit(solution)/shard_map/all_to_all | solution.py:266
  279.4 66.0 %all-gather.5.cloned.1.call-start = ((), (), s32[]{:S(2)}) async-start(), calls=%async_computation.6 | async-start | bytes 2027520 | tf_op jit(solution)/shard_map/all_gather | solution.py:270
  286.8 7.9 collective-permute-start
  290.1 10.8 %collective-permute-start.1 = (bf16[12,128,40]{2,1,0:T(8,128)(2,1)}, bf16[12,128,40]{2,1,0:T(8,128)(2,1)S(1)}, u32[]{:S(2)}, u32[]{:S(2)}) collective-permute-start(bf16[12,128,40]{2,1,0:T(8,128)(2,1)} %get-tuple-element.7), channel_id=1, source_target_pairs={{4,0},{8,4},{12,8},{16,12},{20,16},{24,20},{28,24},{5,1},{9,5},{13... | collective-permute-start | bytes 368648 | tf_op jit(solution)/shard_map/ppermute | solution.py:294
  294.7 57.7 %copy-start.5 = (bf16[12,128,40]{2,1,0:T(8,128)(2,1)}, bf16[12,128,40]{2,1,0:T(8,128)(2,1)S(1)}, u32[]{:S(2)}) copy-start(bf16[12,128,40]{2,1,0:T(8,128)(2,1)S(1)} %collective-permute-done) | copy-start | bytes 368644
  301.0 51.5 %copy-start.7 = (bf16[12,128,40]{2,1,0:T(8,128)(2,1)}, bf16[12,128,40]{2,1,0:T(8,128)(2,1)S(1)}, u32[]{:S(2)}) copy-start(bf16[12,128,40]{2,1,0:T(8,128)(2,1)S(1)} %collective-permute-done.1) | copy-start | bytes 368644
  301.8 86.4 %collective-permute-start.2 = (bf16[12,66,40]{2,1,0:T(8,128)(2,1)}, bf16[12,66,40]{2,1,0:T(8,128)(2,1)}, u32[]{:S(2)}, u32[]{:S(2)}) collective-permute-start(bf16[12,66,40]{2,1,0:T(8,128)(2,1)} %pad_maximum_fusion.2), channel_id=1, source_target_pairs={{0,1},{1,2},{2,3},{4,5},{5,6},{6,7},{8,9},{9,10},{10,11},{12,13},{... | collective-permute-start | bytes 190088 | tf_op jit(solution)/shard_map/ppermute | solution.py:294
  310.9 89.2 %collective-permute-start.3 = (bf16[12,66,40]{2,1,0:T(8,128)(2,1)}, bf16[12,66,40]{2,1,0:T(8,128)(2,1)}, u32[]{:S(2)}, u32[]{:S(2)}) collective-permute-start(bf16[12,66,40]{2,1,0:T(8,128)(2,1)} %pad_maximum_fusion.3), channel_id=1, source_target_pairs={{1,0},{2,1},{3,2},{5,4},{6,5},{7,6},{9,8},{10,9},{11,10},{13,12},{... | collective-permute-start | bytes 190088 | tf_op jit(solution)/shard_map/ppermute | solution.py:294
  393.7 8.3 %copy-start.6 = (bf16[12,128,40]{2,1,0:T(8,128)(2,1)S(1)}, bf16[12,128,40]{2,1,0:T(8,128)(2,1)}, u32[]{:S(2)}) copy-start(bf16[12,128,40]{2,1,0:T(8,128)(2,1)} %copy-done.5) | copy-start | bytes 368644
  393.7 8.3 %copy-start.8 = (bf16[12,128,40]{2,1,0:T(8,128)(2,1)S(1)}, bf16[12,128,40]{2,1,0:T(8,128)(2,1)}, u32[]{:S(2)}) copy-start(bf16[12,128,40]{2,1,0:T(8,128)(2,1)} %copy-done.7) | copy-start | bytes 368644
  520.6 8.9 %copy-start = (bf16[768,128,128]{2,0,1:T(8,128)(2,1)}, bf16[768,128,128]{2,0,1:T(8,128)(2,1)S(1)}, u32[]{:S(2)}) copy-start(bf16[768,128,128]{2,0,1:T(8,128)(2,1)S(1)} %copy.301) | copy-start | bytes 75497472
  520.6 36.6 %copy-start.9 = (bf16[9,128,128]{2,1,0:T(8,128)(2,1)S(1)}, bf16[9,128,128]{2,1,0:T(8,128)(2,1)}, u32[]{:S(2)}) copy-start(bf16[9,128,128]{2,1,0:T(8,128)(2,1)} %param.16) | copy-start | bytes 884740
  530.3 8.1 %all-to-all-start.5 = ((bf16[4,192,128]{2,1,0:T(8,128)(2,1)}), bf16[4,192,128]{2,1,0:T(8,128)(2,1)S(1)}, u32[]{:S(2)}, u32[]{:S(2)}) async-start(bf16[4,192,128]{2,1,0:T(8,128)(2,1)} %bitcast.58), calls=%async_computation.5 | async-start | bytes 393216 | tf_op jit(solution)/shard_map/all_to_all | solution.py:267
  538.4 15.0 %all-to-all-start.4 = ((bf16[8,192,128]{2,1,0:T(8,128)(2,1)}), bf16[8,192,128]{2,1,0:T(8,128)(2,1)S(1)}, u32[]{:S(2)}, u32[]{:S(2)}) async-start(bf16[8,192,128]{2,1,0:T(8,128)(2,1)} %bitcast.55), calls=%async_computation.4 | async-start | bytes 786432 | tf_op jit(solution)/shard_map/all_to_all | solution.py:266
  542.0 86.4 %all-gather.7.cloned.1.call-start = ((), (), s32[]{:S(2)}) async-start(), calls=%async_computation.7 | async-start | bytes 6488064 | tf_op jit(solution)/shard_map/all_gather | solution.py:270
  554.1 20.1 %collective-permute-start.4 = (bf16[12,128,128]{2,1,0:T(8,128)(2,1)S(1)}, bf16[12,128,128]{2,1,0:T(8,128)(2,1)S(1)}, u32[]{:S(2)}, u32[]{:S(2)}) collective-permute-start(bf16[12,128,128]{2,1,0:T(8,128)(2,1)S(1)} %bitcast.261), channel_id=1, source_target_pairs={{0,4},{4,8},{8,12},{12,16},{16,20},{20,24},{24,28},{1,5},{5,9},{9,... | collective-permute-start | bytes 1179656 | tf_op jit(solution)/shard_map/ppermute | solution.py:294
  557.6 16.6 %collective-permute-start.5 = (bf16[12,128,128]{2,1,0:T(8,128)(2,1)S(1)}, bf16[12,128,128]{2,1,0:T(8,128)(2,1)S(1)}, u32[]{:S(2)}, u32[]{:S(2)}) collective-permute-start(bf16[12,128,128]{2,1,0:T(8,128)(2,1)S(1)} %bitcast.262), channel_id=1, source_target_pairs={{4,0},{8,4},{12,8},{16,12},{20,16},{24,20},{28,24},{5,1},{9,5},{13... | collective-permute-start | bytes 1179656 | tf_op jit(solution)/shard_map/ppermute | solution.py:294
  574.2 57.5 %copy-start.1 = (bf16[12,128,128]{2,1,0:T(8,128)(2,1)}, bf16[12,128,128]{2,1,0:T(8,128)(2,1)S(1)}, u32[]{:S(2)}) copy-start(bf16[12,128,128]{2,1,0:T(8,128)(2,1)S(1)} %collective-permute-done.4) | copy-start | bytes 1179652
  574.3 57.5 %copy-start.3 = (bf16[12,128,128]{2,1,0:T(8,128)(2,1)}, bf16[12,128,128]{2,1,0:T(8,128)(2,1)S(1)}, u32[]{:S(2)}) copy-start(bf16[12,128,128]{2,1,0:T(8,128)(2,1)S(1)} %collective-permute-done.5) | copy-start | bytes 1179652
  575.2 85.5 %collective-permute-start.6 = (bf16[12,66,128]{2,1,0:T(8,128)(2,1)}, bf16[12,66,128]{2,1,0:T(8,128)(2,1)}, u32[]{:S(2)}, u32[]{:S(2)}) collective-permute-start(bf16[12,66,128]{2,1,0:T(8,128)(2,1)} %pad_maximum_fusion.4), channel_id=1, source_target_pairs={{0,1},{1,2},{2,3},{4,5},{5,6},{6,7},{8,9},{9,10},{10,11},{12,13},{... | collective-permute-start | bytes 608264 | tf_op jit(solution)/shard_map/ppermute | solution.py:294
  580.8 82.3 %collective-permute-start.7 = (bf16[12,66,128]{2,1,0:T(8,128)(2,1)}, bf16[12,66,128]{2,1,0:T(8,128)(2,1)}, u32[]{:S(2)}, u32[]{:S(2)}) collective-permute-start(bf16[12,66,128]{2,1,0:T(8,128)(2,1)} %pad_maximum_fusion.5), channel_id=1, source_target_pairs={{1,0},{2,1},{3,2},{5,4},{6,5},{7,6},{9,8},{10,9},{11,10},{13,12},{... | collective-permute-start | bytes 608264 | tf_op jit(solution)/shard_map/ppermute | solution.py:294
  657.2 7.7 copy-start.4
  657.2 8.6 %copy-start.2 = (bf16[12,128,128]{2,1,0:T(8,128)(2,1)S(1)}, bf16[12,128,128]{2,1,0:T(8,128)(2,1)}, u32[]{:S(2)}) copy-start(bf16[12,128,128]{2,1,0:T(8,128)(2,1)} %copy-done.1) | copy-start | bytes 1179652
Sparse Core Ops, SparseCore 0:
  286.8 58.5 all-gather.4
  554.2 74.2 all-gather.6

commit v2 on v1

--- a/solution.py
+++ b/solution.py
@@ -11,6 +11,7 @@
 F32 = jnp.float32
 VMEM_LIMIT = 60 * 1024 * 1024
 PAIRS = 8
+UNROLLED = True
 GELU_COEF = (
     0.7978842684146765,
     0.03633414911622174,
@@ -110,18 +111,21 @@
 def conv_kernel(
     first, x_ref, top_ref, bot_ref, left_ref, right_ref, wa_ref, wb_ref, b_ref, out_ref, *scratch
 ):
+    if first:
+        ends, scratch = scratch[0], scratch[1:]
     sl, win = scratch[0], scratch[1]
     rows = out_ref.shape[0] if first else out_ref.shape[2]
     cols = sl.shape[1]
     width = sl.shape[2] // 2
     chan = left_ref.shape[-1]
-
-    def put(pair, parity, row32, lo, hi):
-        win[parity, 8 : 8 + cols, :] = row32
-        win[parity, 7:8, :] = lo
-        win[parity, 8 + cols : 9 + cols, :] = hi
-        before = win[parity, 7 : 7 + cols, :]
-        after = win[parity, 9 : 9 + cols, :]
+    slots = win.shape[0]
+
+    def put(slot, pair, parity, row32, lo, hi):
+        win[slot, 8 : 8 + cols, :] = row32
+        win[slot, 7:8, :] = lo
+        win[slot, 8 + cols : 9 + cols, :] = hi
+        before = win[slot, 7 : 7 + cols, :]
+        after = win[slot, 9 : 9 + cols, :]
         base = parity * width
         if first:
             g = before + pltpu.roll(row32, chan, 1) + pltpu.roll(after, 2 * chan, 1)
@@ -147,57 +151,82 @@
         full = wide(ref[0].astype(F32))
         return full[:cols], full[cols : cols + 1], full[cols + 1 : cols + 2]
 
+    def put_row(r, k):
+        put(
+            k % slots,
+            r // 2 + k % 2 if isinstance(r, int) else (r - k % 2) // 2 + k % 2,
+            1 - k % 2,
+            row_at(r),
+            wide(left_ref[0, pl.ds(r, 1), :]),
+            wide(right_ref[0, pl.ds(r, 1), :]),
+        )
+
     row, lo, hi = halo_row(top_ref)
-    put(0, 0, row, lo, hi)
+    put(0, 0, 0, row, lo, hi)
     row, lo, hi = halo_row(bot_ref)
-    put(rows // 2, 1, row, lo, hi)
-
-    def fill(i, _):
-        for parity in range(2):
-            r = 2 * i + parity
-            put(
-                i + parity,
-                1 - parity,
-                row_at(r),
-                wide(left_ref[0, pl.ds(r, 1), :]),
-                wide(right_ref[0, pl.ds(r, 1), :]),
-            )
+    put(1, rows // 2, 1, row, lo, hi)
+    unroll = UNROLLED
+    n = 2 * PAIRS
+
+    def fill_loop(i, _):
+        for k in range(slots):
+            put_row(i * slots + k, k)
         return 0
 
-    lax.fori_loop(0, rows // 2, fill, 0, unroll=2)
-
-    def chunk(g, _):
-        p0 = g * PAIRS
+    def dots(p0):
         a = sl[pl.ds(p0, PAIRS)].reshape(PAIRS * cols, 2 * width)
         b = sl[pl.ds(p0 + 1, PAIRS)].reshape(PAIRS * cols, 2 * width)
-        y = jnp.dot(a, wa_ref[...], preferred_element_type=F32) + jnp.dot(
+        return jnp.dot(a, wa_ref[...], preferred_element_type=F32) + jnp.dot(
             b, wb_ref[...], preferred_element_type=F32
         )
+
+    def finish(g, y):
+        p0 = g * PAIRS
         hid = y.shape[1] // 2
         if first:
-            y = gelu(y + b_ref[...]).astype(BF)
+            y = gelu(y + b_ref[...])
             for p in range(PAIRS):
                 for q in range(2):
-                    out_ref[2 * (p0 + p) + q] = y[p * cols : (p + 1) * cols, q * hid : (q + 1) * hid]
+                    part = y[p * cols : (p + 1) * cols, q * hid : (q + 1) * hid].astype(BF)
+                    r = 2 * (p0 + p) + q
+                    out_ref[r] = part
+                    ends[0, 0, pl.ds(r, 1), :] = part[:1].astype(F32)
+                    ends[1, 0, pl.ds(r, 1), :] = part[cols - 1 :].astype(F32)
+            return
+        flip = scratch[2].at[g % 2 if unroll else 0]
+        for p in range(PAIRS):
+            for q in range(2):
+                part = y[p * cols : (p + 1) * cols, q * hid : (q + 1) * hid]
+                flip[pl.ds(2 * p + q, hid, stride=n), :] = part.T
+
+        def group(o, _):
+            for j in range(8):
+                v = flip[pl.ds((o * 8 + j) * n, n), :]
+                out_ref[o * 8 + j, 0, pl.ds(g * n, n), :] = gelu(v + b_ref[o * 8 + j]).astype(BF)
+            return 0
+
+        if unroll:
+            for o in range(hid // 8):
+                group(o, 0)
         else:
-            flip = scratch[2]
-            n = 2 * PAIRS
-            for p in range(PAIRS):
-                for q in range(2):
-                    part = y[p * cols : (p + 1) * cols, q * hid : (q + 1) * hid]
-                    flip[pl.ds(2 * p + q, hid, stride=n), :] = part.T
-
-            def finish(o, _):
-                for j in range(8):
-                    oo = o * 8 + j
-                    v = flip[pl.ds(oo * n, n), :]
-                    out_ref[oo, 0, pl.ds(g * n, n), :] = gelu(v + b_ref[oo]).astype(BF)
-                return 0
-
-            lax.fori_loop(0, hid // 8, finish, 0)
-        return 0
-
-    lax.fori_loop(0, rows // (2 * PAIRS), chunk, 0)
+            lax.fori_loop(0, hid // 8, group, 0)
+
+    if unroll:
+        for k in range(min(n + 2, rows)):
+            put_row(k, k)
+        for g in range(rows // n):
+            y = dots(g * PAIRS)
+            for k in range((g + 1) * n + 2, min((g + 2) * n + 2, rows)):
+                put_row(k, k)
+            finish(g, y)
+    else:
+        lax.fori_loop(0, rows // slots, fill_loop, 0)
+
+        def chunk(g, _):
+            finish(g, dots(g * PAIRS))
+            return 0
+
+        lax.fori_loop(0, rows // n, chunk, 0)
 
 
 def conv(first, x, halos, weight, bias, face_count, rows, out_cols):
@@ -220,19 +249,25 @@
     wb = jnp.concatenate(wide[2:], axis=0)
     scratch = [
         pltpu.VMEM((rows // 2 + 1, cols, 2 * width), BF),
-        pltpu.VMEM((2, cols + 16, cols), F32),
+        pltpu.VMEM((8, cols + 16, cols), F32),
     ]
     if first:
         bias_in = jnp.concatenate([bias, bias])[None, :]
         bias_spec = pl.BlockSpec((1, 2 * hid), lambda f: (0, 0))
-        out_shape = jax.ShapeDtypeStruct((face_count * rows, cols, hid), BF)
-        out_spec = pl.BlockSpec((rows, cols, hid), lambda f: (f, 0, 0))
+        out_shape = (
+            jax.ShapeDtypeStruct((face_count * rows, cols, hid), BF),
+            jax.ShapeDtypeStruct((2, face_count, rows, hid), F32),
+        )
+        out_spec = (
+            pl.BlockSpec((rows, cols, hid), lambda f: (f, 0, 0)),
+            pl.BlockSpec((2, 1, rows, hid), lambda f: (0, f, 0, 0)),
+        )
     else:
         bias_in = bias
         bias_spec = pl.BlockSpec(memory_space=pltpu.SMEM)
         out_shape = jax.ShapeDtypeStruct((hid, face_count, rows, cols), BF)
         out_spec = pl.BlockSpec((hid, 1, rows, cols), lambda f: (0, f, 0, 0))
-        scratch.append(pltpu.VMEM((hid * 2 * PAIRS, cols), F32))
+        scratch.append(pltpu.VMEM((2, hid * 2 * PAIRS, cols), F32))
     return pl.pallas_call(
         functools.partial(conv_kernel, first),
         out_shape=out_shape,
@@ -266,28 +301,53 @@
     row_part = lax.all_to_all(row_edge, "band", 0, 0, tiled=True)
     col_part = lax.all_to_all(col_edge, "tile", 0, 0, tiled=True)
     mine = jnp.concatenate([row_part[0], row_part[-1], col_part[0], col_part[-1]], axis=0)
-    rp, cp = row_edge.shape[1], col_edge.shape[1]
     every = lax.all_gather(mine, ("band", "tile"), axis=0, tiled=False)
-    every = every.reshape(nb, nt, 2 * rp + 2 * cp, chan)
-    row_all = every[:, :, : 2 * rp].reshape(nb, nt, 2, rp, chan)
-    row_all = row_all.transpose(2, 0, 3, 1, 4).reshape(2, faces, cols, nt, chan)
-    row_all = row_all.transpose(1, 0, 3, 2, 4).reshape(faces, 2, side, chan)
-    col_all = every[:, :, 2 * rp :].reshape(nb, nt, 2, cp, chan)
-    col_all = col_all.transpose(2, 1, 3, 0, 4).reshape(2, faces, rows, nb, chan)
-    col_all = col_all.transpose(1, 0, 3, 2, 4).reshape(faces, 2, side, chan)
-    lines = jnp.concatenate([row_all, col_all], axis=1).reshape(faces * 4, side, chan)
-    lines = jnp.pad(lines, ((0, 0), (1, 1), (0, 0)))
-
-    def segments(which, start, length):
-        index = seam_table[:, which, 0] * 4 + seam_table[:, which, 1]
-        rev = seam_table[:, which, 2] == 1
-        first = jnp.where(rev, side - start - length, start)
-        got = jax.vmap(
-            lambda i, s: lax.dynamic_slice(lines, (i, s, 0), (1, length + 2, chan))[0]
-        )(index, first)
-        flip = jnp.eye(length + 2, dtype=BF)[::-1]
-        flipped = jnp.einsum("pq,fqc->fpc", flip, got, preferred_element_type=F32).astype(BF)
-        return jnp.where(rev[:, None, None], flipped, got)
+    pieces = every.reshape(-1, rows, chan)
+    per_row, per_col = row_edge.shape[1] // rows, col_edge.shape[1] // rows
+    per_dev = 2 * (per_row + per_col)
+    per_tile = cols // rows
+    last_piece = side // rows - 1
+
+    def wanted(which, first, count):
+        at = first - 1 + jnp.arange(count + 2, dtype=jnp.int32)
+        face = seam_table[:, which, 0][:, None]
+        edge = seam_table[:, which, 1][:, None]
+        rev = seam_table[:, which, 2][:, None] == 1
+        q = jnp.clip(jnp.where(rev, last_piece - at, at), 0, last_piece)
+        c = face * per_tile + q % per_tile
+        on_row = (c // per_row * nt + q // per_tile) * per_dev + edge * per_row + c % per_row
+        on_col = (
+            (q * nt + face // per_col) * per_dev
+            + 2 * per_row
+            + (edge - 2) * per_col
+            + face % per_col
+        )
+        return jnp.where(edge < 2, on_row, on_col), jnp.broadcast_to(rev, q.shape)
+
+    asked = [
+        (0, tile * per_tile, per_tile),
+        (1, tile * per_tile, per_tile),
+        (2, band, 1),
+        (3, band, 1),
+    ]
+    parts = [wanted(*a) for a in asked]
+    index = jnp.concatenate([p[0] for p in parts], axis=1)
+    rev = jnp.concatenate([p[1] for p in parts], axis=1)
+    got = jnp.take(pieces, index.reshape(-1), axis=0, mode="clip")
+    flip = jnp.eye(rows, dtype=BF)[::-1]
+    flipped = jnp.einsum("pq,kqc->kpc", flip, got, preferred_element_type=F32).astype(BF)
+    got = jnp.where(rev.reshape(-1)[:, None, None], flipped, got)
+    got = got.reshape(faces, index.shape[1], rows, chan)
+    offset = [0]
+    for a in asked:
+        offset.append(offset[-1] + a[2] + 2)
+
+    def segments(which):
+        o, n, first = offset[which], asked[which][2], asked[which][1]
+        middle = got[:, o + 1 : o + 1 + n].reshape(faces, n * rows, chan)
+        lead = jnp.where(first > 0, got[:, o, -1:], 0)
+        trail = jnp.where(first + n <= last_piece, got[:, o + 1 + n, :1], 0)
+        return lead, middle, trail
 
     def shift(x, axis, size, forward):
         pairs = [(i, i + 1) if forward else (i + 1, i) for i in range(size - 1)]
@@ -299,16 +359,17 @@
     ext_right = jnp.concatenate([above[:, -1:], right, below[:, -1:]], axis=1)
     from_left = shift(ext_right, "tile", nt, True)
     from_right = shift(ext_left, "tile", nt, False)
-    lefts = jnp.where(tile == 0, segments(2, band * rows, rows), from_left)
-    rights = jnp.where(tile == nt - 1, segments(3, band * rows, rows), from_right)
-
-    def line(at_edge, seam, inner, at):
-        seam = jnp.concatenate([seam[:, 1:-1], seam[:, :1], seam[:, -1:]], axis=1)
-        inner = jnp.concatenate([inner, lefts[:, at : at + 1], rights[:, at : at + 1]], axis=1)
-        return jnp.where(at_edge, seam, inner)
-
-    tops = line(band == 0, segments(0, tile * cols, cols), above, 0)
-    bots = line(band == nb - 1, segments(1, tile * cols, cols), below, rows + 1)
+    lefts = jnp.where(tile == 0, jnp.concatenate(segments(2), axis=1), from_left)
+    rights = jnp.where(tile == nt - 1, jnp.concatenate(segments(3), axis=1), from_right)
+
+    def line(at_edge, which, inner, at):
+        lead, middle, trail = segments(which)
+        lead = jnp.where(at_edge, lead, lefts[:, at : at + 1])
+        trail = jnp.where(at_edge, trail, rights[:, at : at + 1])
+        return jnp.concatenate([jnp.where(at_edge, middle, inner), lead, trail], axis=1)
+
+    tops = line(band == 0, 0, above, 0)
+    bots = line(band == nb - 1, 1, below, rows + 1)
     return tops, bots, lefts[:, 1:-1].astype(F32), rights[:, 1:-1].astype(F32)
 
 
@@ -353,17 +414,20 @@
         arrived_slots.reshape(-1), arrived.reshape(devices * capacity, fields, block_len), slots_dev
     )
     tiles = grid.reshape(faces, rows, fields, block_len)
+    pick = jnp.eye(block_len, dtype=BF)[jnp.array([0, block_len - 1])]
+    ends = jnp.einsum("ep,tcp->etc", pick, grid, preferred_element_type=F32).astype(BF)
+    ends = ends.reshape(2, faces, rows, fields)
     halos = halos_of(
         tiles[:, 0].transpose(0, 2, 1),
         tiles[:, -1].transpose(0, 2, 1),
-        tiles[:, :, :, 0],
-        tiles[:, :, :, -1],
+        ends[0],
+        ends[1],
         seam_table,
     )
-    hidden = conv(True, grid, halos, conv1_weight, conv1_bias, faces, rows, block_len)
+    hidden, ends = conv(True, grid, halos, conv1_weight, conv1_bias, faces, rows, block_len)
     tiles = hidden.reshape(faces, rows, block_len, hidden.shape[2])
     halos = halos_of(
-        tiles[:, 0], tiles[:, -1], tiles[:, :, 0], tiles[:, :, -1], seam_table
+        tiles[:, 0], tiles[:, -1], ends[0].astype(BF), ends[1].astype(BF), seam_table
     )
     return conv(False, hidden, halos, conv2_weight, conv2_bias, faces, rows, block_len)
 

time: 802 us -> 620 us (0.77)
  local copies, waits for them, and re-layouts: 152 us -> 36.3 us
  Pallas kernels: 249 us -> 187 us
    pallas_call x2, Pallas kernels: 219 us -> 156 us  [conv(): pl.pallas_call(functools.partial(conv_kernel, first), out_shape=out_shape...]
    pallas_call x2 -> x0, local copies, waits for them, and re-layouts: 51.8 us -> none  [the longest x1 33.9 us: collect(): pl.pallas_call(collect_kernel, out_shape=jax.ShapeDtypeStruct((slots_dev,...]
    concatenate x2 -> x0, local copies, waits for them, and re-layouts: 16 us -> none  [halos_of(): jnp.concatenate([row_all, col_all], axis=1).reshape(faces * 4, side, chan)]
    pad x2 -> x0, local copies, waits for them, and re-layouts: 13.3 us -> none  [halos_of(): lines = jnp.pad(lines, ((0, 0), (1, 1), (0, 0)))]
    unnamed x31 -> x23, local copies, waits for them, and re-layouts: 11.6 us -> 1.59 us
    gather x8 -> x4, local copies, waits for them, and re-layouts: 19.8 us -> 9.84 us  [the longest x3 9.28 us: halos_of(): got = jnp.take(pieces, index.reshape(-1), axis=0, mode='clip')]
    transpose x8 -> x0, local copies, waits for them, and re-layouts: 9.36 us -> none  [the longest x2 3.78 us: halos_of(): col_all = col_all.transpose(2, 1, 3, 0, 4).reshape(2, faces, rows, nb, chan)]
    slice x17 -> x7, local copies, waits for them, and re-layouts: 9.82 us -> 1.76 us  [the longest x1 0.98 us: local(): tiles[:, -1].transpose(0, 2, 1)]
  transfers between devices with their start and end apart: 16 -> 16, of which waited for: 9 -> 10; matrix products, arithmetic and copies ran while one was open for 13% -> 8% of each run, Pallas kernels for 2% -> 3%
where the time goes in v2:
time: 620 us; the launch traced here: 618 us
  waiting for transfers between devices  291 us (47%)
  Pallas kernels  187 us (30%)
  starting transfers between devices  56.3 us (9%)
  local copies, waits for them, and re-layouts  36.3 us (6%)
  other arithmetic  25.1 us (4%)
  between operations  14.1 us (2%)
  matrix products  8.59 us (1%)
    all_to_all x1, waiting for transfers between devices, local(): lax.all_to_all(outgoing.reshape(devices, capacity, fields, block_len), ax...  171 us
    pallas_call x2, Pallas kernels, conv(): pl.pallas_call(functools.partial(conv_kernel, first), out_shape=out_shape...  156 us
    all_gather x2, waiting for transfers between devices, halos_of(): every = lax.all_gather(mine, ('band', 'tile'), axis=0, tiled=False)  76.9 us
    ppermute x8, starting transfers between devices, shift(): return lax.ppermute(x, axis, pairs)  25.7 us
    ppermute x8, waiting for transfers between devices, shift(): return lax.ppermute(x, axis, pairs)  25.6 us
    pallas_call x1, Pallas kernels, partials(): pl.pallas_call(partial_kernel, out_shape=jax.ShapeDtypeStruct((slots, fie...  16.2 us
    all_to_all x2, waiting for transfers between devices, halos_of(): row_part = lax.all_to_all(row_edge, 'band', 0, 0, tiled=True)  15.5 us
    pallas_call x1, Pallas kernels, collect(): pl.pallas_call(collect_kernel, out_shape=jax.ShapeDtypeStruct((slots_dev,...  14 us
  transfers between devices with their start and end apart: 16, of which 10 were waited for; matrix products, arithmetic and copies ran while one was open for 8% of the time, Pallas kernels for 3%

profile of v2, /device:TPU:1, one launch (start us, length us, event | category | flops | bytes accessed | tf_op | source)
XLA Modules:
  0.0 618.3 jit_solution(5980821920272036998)
XLA Ops:
  9.4 7.1 %all-to-all-start = ((s32[32,1,24]{2,1,0:T(1,128)}), s32[32,1,24]{2,1,0:T(1,128)S(1)}, u32[]{:S(2)}, u32[]{:S(2)}) async-start(s32[32,1,24]{2,1,0:T(1,128)} %bitcast), calls=%async_computation | async-start | bytes 32768 | tf_op jit(solution)/shard_map/all_to_all | solution.py:410
  16.5 16.2 %partials.1 = bf16[768,40,128]{2,1,0:T(8,128)(2,1)} custom-call(s32[256]{0:T(256)} %copy-done.6, bf16[40,8192]{1,0:T(8,128)(2,1)} %src_ref.1, bf16[64,4,128,128]{3,2,1,0:T(8,128)(2,1)} %w_ref.1), custom_call_target="tpu_custom_call" | custom-call | tf_op jit(solution)/shard_map/partials/pallas_call | solution.py:56
  32.8 5.9 all-to-all-start.1
  41.2 170.7 %all-to-all-done.1 = bf16[32,24,40,128]{3,2,1,0:T(8,128)(2,1)} async-done(((bf16[32,24,40,128]{3,2,1,0:T(8,128)(2,1)}), bf16[32,24,40,128]{3,2,1,0:T(8,128)(2,1)}, u32[]{:S(2)}, u32[]{:S(2)}) %all-to-all-start.1) | async-done | bytes 7864352 | tf_op jit(solution)/shard_map/all_to_all | solution.py:407
  211.8 14.0 %collect.1.x_ref = bf16[768,40,128]{2,1,0:T(8,128)(2,1)} custom-call(s32[768]{0:T(1024)} %reshape.782.slot_ref, bf16[768,40,128]{2,1,0:T(8,128)(2,1)} %bitcast.2.arr_ref), custom_call_target="tpu_custom_call" | custom-call | tf_op jit(solution)/shard_map/collect/pallas_call | solution.py:96
  225.8 5.4 fusion.4
  232.4 4.2 all-to-all-start.3
  239.9 6.5 %all-to-all-start.2 = ((bf16[8,192,40]{1,2,0:T(8,128)(2,1)}), bf16[8,192,40]{1,2,0:T(8,128)(2,1)S(1)}, u32[]{:S(2)}, u32[]{:S(2)}) async-start(bf16[8,192,40]{1,2,0:T(8,128)(2,1)} %copy.487), calls=%async_computation.2 | async-start | bytes 327680 | tf_op jit(solution)/shard_map/all_to_all | solution.py:301
  246.4 6.5 %all-to-all-done.2 = bf16[8,192,40]{1,2,0:T(8,128)(2,1)S(1)} async-done(((bf16[8,192,40]{1,2,0:T(8,128)(2,1)}), bf16[8,192,40]{1,2,0:T(8,128)(2,1)S(1)}, u32[]{:S(2)}, u32[]{:S(2)}) %all-to-all-start.2) | async-done | bytes 122912 | tf_op jit(solution)/shard_map/all_to_all | solution.py:301
  258.1 4.0 collective-permute-start
  262.1 3.3 collective-permute-done.1
  265.4 9.3 %collective-permute-done = bf16[12,128,40]{2,1,0:T(8,128)(2,1)S(1)} collective-permute-done((bf16[12,128,40]{2,1,0:T(8,128)(2,1)S(1)}, bf16[12,128,40]{2,1,0:T(8,128)(2,1)S(1)}, u32[]{:S(2)}, u32[]{:S(2)}) %collective-permute-start) | collective-permute-done | bytes 122912 | tf_op jit(solution)/shard_map/ppermute | solution.py:354
  275.6 2.4 collective-permute-start.3
  278.9 3.3 collective-permute-start.2
  282.1 31.0 %all-gather.5.cloned.1.call-done = bf16[24576,40]{0,1:T(8,128)(2,1)} async-done(((bf16[768,40]{0,1:T(8,128)(2,1)}), bf16[24576,40]{0,1:T(8,128)(2,1)}) %all-gather.5.cloned.1.call-update) | async-done | bytes 1966096 | tf_op jit(solution)/shard_map/all_gather | solution.py:304
  313.1 6.7 %reshape.787 = bf16[384,64,40]{1,0,2:T(8,128)(2,1)} reshape(bf16[24576,40]{0,1:T(8,128)(2,1)} %all-gather.5.cloned.1.call-done) | data formatting | bytes 3932160 | tf_op jit(solution)/shard_map/reshape | solution.py:305
  319.8 6.5 %copy.490 = bf16[384,64,40]{1,2,0:T(8,128)(2,1)} copy(bf16[384,64,40]{1,0,2:T(8,128)(2,1)} %reshape.787) | data formatting | bytes 3932160 | tf_op jit(solution)/shard_map/reshape | solution.py:305
  326.4 3.1 gather_fusion.1
  329.5 2.1 copy.491
  333.2 3.3 copy.493
  343.9 66.2 %conv1.1 = (bf16[768,128,128]{2,1,0:T(8,128)(2,1)}, f32[2,12,64,128]{3,2,1,0:T(8,128)}) custom-call(bf16[768,40,128]{2,1,0:T(8,128)(2,1)} %collect.1.x_ref, bf16[12,130,40]{2,1,0:T(8,128)(2,1)} %pad_maximum_fusion.top_ref, bf16[12,130,40]{2,1,0:T(8,128)(2,1)} %pad_maximum_fusion.1.bot_ref, f32[12,64,40]{2,1,0:T(8,128)} %slice_convert_fusion.5.left_ref, ...), custom_call_target="tpu_custom_call" | custom-call | tf_op jit(solution)/shard_map/conv1/pallas_call | solution.py:271
  412.1 3.4 all-to-all-start.5
  415.4 1.9 bitcast_select_fusion.1
  419.1 3.6 all-to-all-start.4
  422.8 9.1 %all-to-all-done.4 = bf16[8,192,128]{2,1,0:T(8,128)(2,1)S(1)} async-done(((bf16[8,192,128]{2,1,0:T(8,128)(2,1)}), bf16[8,192,128]{2,1,0:T(8,128)(2,1)S(1)}, u32[]{:S(2)}, u32[]{:S(2)}) %all-to-all-start.4) | async-done | bytes 393248 | tf_op jit(solution)/shard_map/all_to_all | solution.py:301
  433.8 3.4 collective-permute-start.4
  439.7 13.0 %collective-permute-done.4 = bf16[12,128,128]{2,1,0:T(8,128)(2,1)S(1)} collective-permute-done((bf16[12,128,128]{2,1,0:T(8,128)(2,1)S(1)}, bf16[12,128,128]{2,1,0:T(8,128)(2,1)S(1)}, u32[]{:S(2)}, u32[]{:S(2)}) %collective-permute-start.4) | collective-permute-done | bytes 393248 | tf_op jit(solution)/shard_map/ppermute | solution.py:354
  453.6 5.5 collective-permute-start.7
  459.8 4.5 collective-permute-start.6
  464.3 45.9 %all-gather.7.cloned.1.call-done = bf16[24576,128]{1,0:T(8,128)(2,1)} async-done(((bf16[768,128]{1,0:T(8,128)(2,1)}), bf16[24576,128]{1,0:T(8,128)(2,1)}) %all-gather.7.cloned.1.call-update) | async-done | bytes 6291472 | tf_op jit(solution)/shard_map/all_gather | solution.py:304
  510.2 4.0 gather_fusion.2
  521.4 90.1 %conv2.1 = bf16[128,12,64,128]{3,2,1,0:T(8,128)(2,1)} custom-call(bf16[768,128,128]{2,1,0:T(8,128)(2,1)} %get-tuple-element.7.x_ref, bf16[12,130,128]{2,1,0:T(8,128)(2,1)} %pad_maximum_fusion.2.top_ref, bf16[12,130,128]{2,1,0:T(8,128)(2,1)} %pad_maximum_fusion.3.bot_ref, f32[12,64,128]{2,1,0:T(8,128)} %slice_convert_fusion.3.left_ref, ...), custom_call_target="tpu_custom_call" | custom-call | tf_op jit(solution)/shard_map/conv2/pallas_call | solution.py:271
  (134 shorter events, 42.3 us)
Async XLA Ops:
  8.5 8.0 %copy-start.6 = (s32[256]{0:T(256)}, s32[256]{0:T(256)S(1)}, u32[]{:S(2)}) copy-start(s32[256]{0:T(256)S(1)} %convert_add_fusion.pos_ref) | copy-start | bytes 3076
  9.4 23.3 %all-to-all-start = ((s32[32,1,24]{2,1,0:T(1,128)}), s32[32,1,24]{2,1,0:T(1,128)S(1)}, u32[]{:S(2)}, u32[]{:S(2)}) async-start(s32[32,1,24]{2,1,0:T(1,128)} %bitcast), calls=%async_computation | async-start | bytes 32768 | tf_op jit(solution)/shard_map/all_to_all | solution.py:410
  32.8 179.0 %all-to-all-start.1 = ((bf16[32,24,40,128]{3,2,1,0:T(8,128)(2,1)}), bf16[32,24,40,128]{3,2,1,0:T(8,128)(2,1)}, u32[]{:S(2)}, u32[]{:S(2)}) async-start(bf16[32,24,40,128]{3,2,1,0:T(8,128)(2,1)} %bitcast.207), calls=%async_computation.1 | async-start | bytes 15728640 | tf_op jit(solution)/shard_map/all_to_all | solution.py:407
  231.2 22.5 %copy-start.4 = (s32[12,4,3]{0,1,2:T(4,128)S(1)}, s32[12,4,3]{0,1,2:T(4,128)}, u32[]{:S(2)}) copy-start(s32[12,4,3]{0,1,2:T(4,128)} %param.14) | copy-start | bytes 1732
  231.2 23.4 %copy-start.3 = (bf16[9,128,40]{1,2,0:T(8,128)(2,1)S(1)}, bf16[9,128,40]{1,2,0:T(8,128)(2,1)}, u32[]{:S(2)}) copy-start(bf16[9,128,40]{1,2,0:T(8,128)(2,1)} %param.15) | copy-start | bytes 276484
  231.2 24.7 %copy-start.8 = (f32[128]{0:T(128)S(1)}, f32[128]{0:T(128)}, u32[]{:S(2)}) copy-start(f32[128]{0:T(128)} %param.16) | copy-start | bytes 1540
  232.4 7.5 %all-to-all-start.3 = ((bf16[4,192,40]{1,2,0:T(8,128)(2,1)}), bf16[4,192,40]{1,2,0:T(8,128)(2,1)S(1)}, u32[]{:S(2)}, u32[]{:S(2)}) async-start(bf16[4,192,40]{1,2,0:T(8,128)(2,1)} %copy.489), calls=%async_computation.3 | async-start | bytes 163840 | tf_op jit(solution)/shard_map/all_to_all | solution.py:302
  239.9 13.0 %all-to-all-start.2 = ((bf16[8,192,40]{1,2,0:T(8,128)(2,1)}), bf16[8,192,40]{1,2,0:T(8,128)(2,1)S(1)}, u32[]{:S(2)}, u32[]{:S(2)}) async-start(bf16[8,192,40]{1,2,0:T(8,128)(2,1)} %copy.487), calls=%async_computation.2 | async-start | bytes 327680 | tf_op jit(solution)/shard_map/all_to_all | solution.py:301
  246.3 66.8 %all-gather.5.cloned.1.call-start = ((), (), s32[]{:S(2)}) async-start(), calls=%async_computation.6 | async-start | bytes 2027520 | tf_op jit(solution)/shard_map/all_gather | solution.py:304
  254.5 71.9 %copy-start.5 = (s32[1024]{0:T(1024)}, s32[1024]{0:T(1024)S(1)}, u32[]{:S(2)}) copy-start(s32[1024]{0:T(1024)S(1)} %pad_clamp_fusion) | copy-start | bytes 12292
  254.6 10.9 %collective-permute-start.1 = (bf16[12,128,40]{2,1,0:T(8,128)(2,1)S(1)}, bf16[12,128,40]{2,1,0:T(8,128)(2,1)S(1)}, u32[]{:S(2)}, u32[]{:S(2)}) collective-permute-start(bf16[12,128,40]{2,1,0:T(8,128)(2,1)S(1)} %bitcast.218), channel_id=1, source_target_pairs={{4,0},{8,4},{12,8},{16,12},{20,16},{24,20},{28,24},{5,1},{9,5},{13... | collective-permute-start | bytes 368648 | tf_op jit(solution)/shard_map/ppermute | solution.py:354
  258.1 16.6 %collective-permute-start = (bf16[12,128,40]{2,1,0:T(8,128)(2,1)S(1)}, bf16[12,128,40]{2,1,0:T(8,128)(2,1)S(1)}, u32[]{:S(2)}, u32[]{:S(2)}) collective-permute-start(bf16[12,128,40]{2,1,0:T(8,128)(2,1)S(1)} %bitcast.217), channel_id=1, source_target_pairs={{0,4},{4,8},{8,12},{12,16},{16,20},{20,24},{24,28},{1,5},{5,9},{9,... | collective-permute-start | bytes 368648 | tf_op jit(solution)/shard_map/ppermute | solution.py:354
  274.7 45.1 %copy-start = (bf16[12,128,40]{2,1,0:T(8,128)(2,1)}, bf16[12,128,40]{2,1,0:T(8,128)(2,1)S(1)}, u32[]{:S(2)}) copy-start(bf16[12,128,40]{2,1,0:T(8,128)(2,1)S(1)} %collective-permute-done) | copy-start | bytes 368644
  275.6 64.2 %collective-permute-start.3 = (bf16[12,66,40]{2,1,0:T(8,128)(2,1)}, bf16[12,66,40]{2,1,0:T(8,128)(2,1)}, u32[]{:S(2)}, u32[]{:S(2)}) collective-permute-start(bf16[12,66,40]{2,1,0:T(8,128)(2,1)} %pad_maximum_fusion.5), channel_id=1, source_target_pairs={{1,0},{2,1},{3,2},{5,4},{6,5},{7,6},{9,8},{10,9},{11,10},{13,12},{... | collective-permute-start | bytes 190088 | tf_op jit(solution)/shard_map/ppermute | solution.py:354
  278.9 58.7 %collective-permute-start.2 = (bf16[12,66,40]{2,1,0:T(8,128)(2,1)}, bf16[12,66,40]{2,1,0:T(8,128)(2,1)}, u32[]{:S(2)}, u32[]{:S(2)}) collective-permute-start(bf16[12,66,40]{2,1,0:T(8,128)(2,1)} %pad_maximum_fusion.4), channel_id=1, source_target_pairs={{0,1},{1,2},{2,3},{4,5},{5,6},{6,7},{8,9},{9,10},{10,11},{12,13},{... | collective-permute-start | bytes 190088 | tf_op jit(solution)/shard_map/ppermute | solution.py:354
  329.5 2.2 copy-start.7
  338.6 4.4 copy-start.1
  410.2 27.1 %copy-start.2 = (bf16[9,128,128]{2,1,0:T(8,128)(2,1)S(1)}, bf16[9,128,128]{2,1,0:T(8,128)(2,1)}, u32[]{:S(2)}) copy-start(bf16[9,128,128]{2,1,0:T(8,128)(2,1)} %param.17) | copy-start | bytes 884740
  412.1 7.1 %all-to-all-start.5 = ((bf16[4,192,128]{2,1,0:T(8,128)(2,1)}), bf16[4,192,128]{2,1,0:T(8,128)(2,1)S(1)}, u32[]{:S(2)}, u32[]{:S(2)}) async-start(bf16[4,192,128]{2,1,0:T(8,128)(2,1)} %bitcast.68), calls=%async_computation.5 | async-start | bytes 393216 | tf_op jit(solution)/shard_map/all_to_all | solution.py:302
  419.1 12.7 %all-to-all-start.4 = ((bf16[8,192,128]{2,1,0:T(8,128)(2,1)}), bf16[8,192,128]{2,1,0:T(8,128)(2,1)S(1)}, u32[]{:S(2)}, u32[]{:S(2)}) async-start(bf16[8,192,128]{2,1,0:T(8,128)(2,1)} %bitcast.65), calls=%async_computation.4 | async-start | bytes 786432 | tf_op jit(solution)/shard_map/all_to_all | solution.py:301
  422.7 87.5 %all-gather.7.cloned.1.call-start = ((), (), s32[]{:S(2)}) async-start(), calls=%async_computation.7 | async-start | bytes 6488064 | tf_op jit(solution)/shard_map/all_gather | solution.py:304
  433.8 19.0 %collective-permute-start.4 = (bf16[12,128,128]{2,1,0:T(8,128)(2,1)S(1)}, bf16[12,128,128]{2,1,0:T(8,128)(2,1)S(1)}, u32[]{:S(2)}, u32[]{:S(2)}) collective-permute-start(bf16[12,128,128]{2,1,0:T(8,128)(2,1)S(1)} %get-tuple-element.17), channel_id=1, source_target_pairs={{0,4},{4,8},{8,12},{12,16},{16,20},{20,24},{24,28},{1,5},{5,9},{9,... | collective-permute-start | bytes 1179656 | tf_op jit(solution)/shard_map/ppermute | solution.py:354
  437.4 15.3 %collective-permute-start.5 = (bf16[12,128,128]{2,1,0:T(8,128)(2,1)S(1)}, bf16[12,128,128]{2,1,0:T(8,128)(2,1)S(1)}, u32[]{:S(2)}, u32[]{:S(2)}) collective-permute-start(bf16[12,128,128]{2,1,0:T(8,128)(2,1)S(1)} %get-tuple-element.18), channel_id=1, source_target_pairs={{4,0},{8,4},{12,8},{16,12},{20,16},{24,20},{28,24},{5,1},{9,5},{13... | collective-permute-start | bytes 1179656 | tf_op jit(solution)/shard_map/ppermute | solution.py:354
  453.6 62.3 %collective-permute-start.7 = (bf16[12,66,128]{2,1,0:T(8,128)(2,1)}, bf16[12,66,128]{2,1,0:T(8,128)(2,1)}, u32[]{:S(2)}, u32[]{:S(2)}) collective-permute-start(bf16[12,66,128]{2,1,0:T(8,128)(2,1)} %pad_maximum_fusion.7), channel_id=1, source_target_pairs={{1,0},{2,1},{3,2},{5,4},{6,5},{7,6},{9,8},{10,9},{11,10},{13,12},{... | collective-permute-start | bytes 608264 | tf_op jit(solution)/shard_map/ppermute | solution.py:354
  459.8 57.9 %collective-permute-start.6 = (bf16[12,66,128]{2,1,0:T(8,128)(2,1)}, bf16[12,66,128]{2,1,0:T(8,128)(2,1)}, u32[]{:S(2)}, u32[]{:S(2)}) collective-permute-start(bf16[12,66,128]{2,1,0:T(8,128)(2,1)} %pad_maximum_fusion.6), channel_id=1, source_target_pairs={{0,1},{1,2},{2,3},{4,5},{5,6},{6,7},{8,9},{9,10},{10,11},{12,13},{... | collective-permute-start | bytes 608264 | tf_op jit(solution)/shard_map/ppermute | solution.py:354
Sparse Core Ops, SparseCore 0:
  253.7 59.3 all-gather.4
  432.7 77.4 all-gather.6
